TPU v7x, 32 devices: a whole 2x2x4 slice. The times are simulated.
32 devices in a mesh: draws: 2 (over x), spec: 16 (over z, y, core).
Axes of the slice: x: 2, y: 2, z: 4, core: 2. Of those that a mesh axis runs over, the one named last changes fastest.
Arguments:
- coefficients: bfloat16 [1280, 2, 320, 128], P('draws', None, 'spec'), parts along dimension 0, may hold values from -6 to 6
- legendre: float32 [640, 2, 320, 16], P('spec'), as said below
- row_counts: int32 [16], P('spec'), may hold values from 640 to 1280, as said below
- basis: float32 [64, 128], replicated, may hold values from -0.75 to 0.75
- absorb: float32 [128], replicated, may hold values from 0.00390625 to 0.0625
- peak_level: int32 [512], replicated, may hold values from 0 to 127
- width: float32 [512], replicated, may hold values from 1.5 to 12
Outputs:
- radiance: float32 [32, 2, 1280, 512], P(('draws', 'spec')), parts along dimension 0
There are 2 independent parts, one for each index of `draws`. A program takes and returns all parts, laid end to end along the dimension named above; an argument that names none is the same for every part. Nothing has to cross between parts.
Inputs may be any that keep to these rules, and one draw needn't show every extreme that they name: `legendre`: entry [m, p, s, j] is the associated Legendre function of order m and degree m + 2 s + p, normalised to unit square integral over [-1, 1], at the cosine of a drawn colatitude of row j in the northern hemisphere; it is zero where the degree exceeds 640 - 1. `row_counts`: every count is a multiple of 4; row 0 has 1280 longitudes and row 1 has 640.
All inputs are finite; a program needn't handle non-finite values.
Results may differ from a plain program's by a relative error of at most 0.0003.
Values sent between devices are 32-bit elements; how exact they have to be, the bound alone decides.
A program may use at most 128 MiB of HBM per device.

v0:
```python
import math

import jax
import jax.numpy as jnp
from jax import lax
from jax.sharding import PartitionSpec as P

NLON = 1280


PRECISE = lax.Precision.HIGHEST


def prior_scale(shard, first):
    waves = shard.shape[0]
    slots = shard.shape[2]
    orders = jnp.arange(waves, dtype=jnp.int32)[:, None, None]
    parity = jnp.arange(2, dtype=jnp.int32)[None, :, None]
    slot_index = first + jnp.arange(slots, dtype=jnp.int32)[None, None, :]
    degree = orders + 2 * slot_index + parity
    spread = lax.rsqrt((degree + 1).astype(jnp.float32) * waves)
    spread = jnp.where(degree < waves, spread, jnp.zeros_like(spread))
    return shard.astype(jnp.float32) * spread[..., None]


def channel_kernel(peak_level, width, levels):
    height = jnp.arange(levels, dtype=jnp.float32)[:, None]
    offsets = (height - peak_level.astype(jnp.float32)[None, :]) / width[None, :]
    weights = jnp.exp(-offsets * offsets)
    return weights / jnp.sum(weights, axis=0, keepdims=True)


def radiate(temps, absorb, kernel):
    levels = temps.shape[-1]
    strict_upper = (jnp.arange(levels)[:, None] < jnp.arange(levels)[None, :]).astype(jnp.float32)
    source = jnp.exp(0.5 * temps)
    layers = absorb[None, :] * source
    overhead = jnp.dot(layers, strict_upper, precision=PRECISE, preferred_element_type=jnp.float32)
    emitted = source * jnp.exp(-overhead) * -jnp.expm1(-layers)
    return jnp.dot(emitted, kernel, precision=PRECISE, preferred_element_type=jnp.float32)


def fourier_lookup(row_count, waves, points):
    orders = jnp.arange(waves, dtype=jnp.int32)
    places = jnp.arange(points, dtype=jnp.int32)
    phases = places[:, None] * orders[None, :] % row_count
    angles = 2.0 * math.pi * phases.astype(jnp.float32) / row_count.astype(jnp.float32)
    weights = jnp.where(orders == 0, 1.0, 2.0) * (2 * orders < row_count).astype(jnp.float32)
    return jnp.stack((weights * jnp.cos(angles), -weights * jnp.sin(angles)), axis=-1)


def synthesize_row(spectra, row_count, modes_basis, absorb, kernel, points):
    waves, hemis, columns = spectra.shape
    lookup = fourier_lookup(row_count, waves, points)
    split_parts = spectra.reshape(waves, hemis, 2, columns // 2)
    fields = jnp.einsum("kmq,mhqc->hkc", lookup, split_parts, precision=PRECISE)
    fields = jnp.einsum("hkc,cl->hkl", fields, modes_basis, precision=PRECISE)
    levels = fields.shape[-1]
    bright = radiate(fields.reshape(hemis * points, levels), absorb, kernel)
    bright = bright.reshape(hemis, points, kernel.shape[1])
    inside = (jnp.arange(points, dtype=jnp.int32) < row_count).astype(jnp.float32)
    return bright * inside[None, :, None]


def synthesize_rows(pieces, row_counts, modes_basis, absorb, kernel):
    results = [synthesize_row(pieces[:, :, 0, :], row_counts[0], modes_basis, absorb, kernel, NLON)]
    return jnp.stack(results, axis=0)


def legendre_rows(legendre, spectral):
    even_odd = jnp.einsum("mpsj,mpsc->mpjc", legendre, spectral, precision=PRECISE)
    return jnp.stack((even_odd[:, 0] + even_odd[:, 1], even_odd[:, 0] - even_odd[:, 1]), axis=1)


def on_device(coefficients, legendre, row_counts, basis, absorb, peak_level, width):
    first = lax.axis_index("spec") * coefficients.shape[2]
    scaled = prior_scale(coefficients, first)
    kernel = channel_kernel(peak_level, width, basis.shape[1])
    spectral = lax.all_to_all(scaled, "spec", split_axis=0, concat_axis=2, tiled=True)
    fourier = legendre_rows(legendre, spectral)
    return synthesize_rows(
        lax.all_to_all(fourier, "spec", split_axis=2, concat_axis=0, tiled=True),
        row_counts,
        basis,
        absorb,
        kernel,
    )


def solution(mesh):
    placed = (
        P("draws", None, "spec", None),
        P("spec", None, None, None),
        P("spec"),
        P(),
        P(),
        P(),
        P(),
    )
    return jax.shard_map(
        on_device,
        mesh=mesh,
        in_specs=placed,
        out_specs=P(("draws", "spec"), None, None, None),
        check_vma=False,
    )
```

profile of v0, /device:TPU:0, one launch (start us, length us, event | category | flops | bytes accessed | tf_op | source)
XLA Modules:
  0.0 469.2 jit_solution(60947047972407609)
XLA Ops:
  0.0 0.0 copy-start
  0.0 0.0 copy-start.1
  0.1 2.2 rsqrt_select_fusion
  2.3 0.8 copy-done.1
  3.0 16.7 %convert_multiply_fusion = f32[640,2,20,128]{3,1,2,0:T(2,128)} fusion(bf16[640,2,20,128]{3,1,2,0:T(2,128)(2,1)S(1)} %copy-done.1, f32[640,2,20]{1,2,0:T(8,128)S(1)} %rsqrt_select_fusion), kind=kLoop, calls=%fused_computation.2 | loop fusion | flops 6553600 | bytes 19763200 | tf_op jit(solution)/shard_map/mul | solution.py:23
  19.8 7.5 %all-to-all-start = ((f32[640,2,20,128]{3,1,2,0:T(2,128)}), f32[640,2,20,128]{3,1,2,0:T(2,128)}, u32[]{:S(2)}, u32[]{:S(2)}) async-start(f32[640,2,20,128]{3,1,2,0:T(2,128)} %convert_multiply_fusion), calls=%async_computation | async-start | bytes 26214400 | tf_op jit(solution)/shard_map/all_to_all | solution.py:79
  27.9 232.1 %all-to-all-done = f32[640,2,20,128]{3,1,2,0:T(2,128)} async-done(((f32[640,2,20,128]{3,1,2,0:T(2,128)}), f32[640,2,20,128]{3,1,2,0:T(2,128)}, u32[]{:S(2)}, u32[]{:S(2)}) %all-to-all-start) | async-done | bytes 13107232 | tf_op jit(solution)/shard_map/all_to_all | solution.py:79
  260.0 12.0 %copy.29 = f32[640,2,20,128]{3,0,2,1:T(8,128)} copy(f32[640,2,20,128]{3,1,2,0:T(2,128)} %all-to-all-done) | data formatting | bytes 26214400 | tf_op jit(solution)/shard_map/all_to_all | solution.py:79
  272.0 11.0 %copy.30 = f32[40,2,16,20,128]{4,0,3,2,1:T(8,128)} copy(f32[40,2,16,20,128]{4,0,2,3,1:T(8,128)} %bitcast.37) | data formatting | bytes 26214400 | tf_op jit(solution)/shard_map/all_to_all | solution.py:79
  283.0 0.0 copy-done
  283.0 13.6 %fusion.19 = f32[40,2,16,128]{3,2,1,0:T(8,128)S(1)} fusion(f32[40,2,320,16]{2,3,1,0:T(8,128)S(1)} %copy-done, f32[40,2,320,128]{3,0,2,1:T(8,128)} %bitcast.38), kind=kOutput, calls=%fused_computation.31 | convolution fusion | flops 629145600 | bytes 15400960 | tf_op jit(solution)/shard_map/mpsj,mpsc->mpjc/dot_general | solution.py:71
  296.8 0.0 copy-start.5
  296.8 0.0 copy-start.4
  296.8 1.2 copy.32
  298.0 55.9 %all-to-all-start.1 = ((f32[40,2,16,128]{3,1,0,2:T(2,128)}), f32[40,2,16,128]{3,1,0,2:T(2,128)S(1)}, u32[]{:S(2)}, u32[]{:S(2)}) async-start(f32[40,2,16,128]{3,1,0,2:T(2,128)} %copy.32), calls=%async_computation.1 | async-start | bytes 1310720 | tf_op jit(solution)/shard_map/all_to_all | solution.py:82
  353.9 43.5 %cosine_multiply_fusion = f32[1280,640,1]{1,0,2:T(8,128)} fusion(f32[640]{0:T(1024)S(1)} %get-tuple-element.7, f32[]{:T(128)S(6)} %convert_element_type.42, pred[]{:T(512)S(6)} %lt.70, s32[]{:T(128)S(6)} %select_n.41), kind=kLoop, calls=%fused_computation.19 | loop fusion | flops 9830400 | bytes 3279369 | tf_op jit(solution)/shard_map/mul | solution.py:49
  397.4 0.0 copy-done.5
  397.4 0.0 copy-done.4
  397.4 0.1 fusion.26
  397.5 43.8 %sine_multiply_fusion = f32[1280,640,1]{1,0,2:T(8,128)} fusion(f32[640]{0:T(1024)S(1)} %get-tuple-element.8, f32[]{:T(128)S(6)} %convert_element_type.42, pred[]{:T(512)S(6)} %lt.70, s32[]{:T(128)S(6)} %select_n.41), kind=kLoop, calls=%fused_computation.18 | loop fusion | flops 9830400 | bytes 3279369 | tf_op jit(solution)/shard_map/mul | solution.py:49
  441.3 0.0 all-to-all-done.1
  441.3 0.0 copy-start.2
  441.4 0.8 copy-done.2
  442.2 2.3 reshape.184
  444.4 0.0 copy-start.3
  444.5 0.0 copy-start.6
  444.5 13.5 %fusion.17 = f32[2,1280,64]{1,2,0:T(8,128)S(1)} fusion(f32[1280,640,1]{1,0,2:T(8,128)} %sine_multiply_fusion, f32[1280,640,1]{1,0,2:T(8,128)} %cosine_multiply_fusion, f32[640,2,2,64]{3,2,1,0:T(2,128)S(1)} %reshape.184), kind=kOutput, calls=%fused_computation.28 | convolution fusion | flops 2518220800 | bytes 7864320 | tf_op jit(solution)/shard_map/kmq,mhqc->hkc/dot_general | solution.py:56
  458.0 0.0 copy-done.3
  458.0 2.4 fusion.16
  460.5 0.0 copy-done.6
  460.5 0.1 bitcast_multiply_fusion
  460.6 1.2 fusion.8
  461.8 4.5 fusion.23
  466.2 2.8 broadcast_multiply_fusion
  (7 shorter events, 0.1 us)
Async XLA Ops:
  0.0 283.0 %copy-start = (f32[40,2,320,16]{2,3,1,0:T(8,128)S(1)}, f32[40,2,320,16]{2,3,1,0:T(8,128)}, u32[]{:S(2)}) copy-start(f32[40,2,320,16]{2,3,1,0:T(8,128)} %param.8) | copy-start | bytes 4915204
  0.0 3.0 copy-start.1
  19.8 240.2 %all-to-all-start = ((f32[640,2,20,128]{3,1,2,0:T(2,128)}), f32[640,2,20,128]{3,1,2,0:T(2,128)}, u32[]{:S(2)}, u32[]{:S(2)}) async-start(f32[640,2,20,128]{3,1,2,0:T(2,128)} %convert_multiply_fusion), calls=%async_computation | async-start | bytes 26214400 | tf_op jit(solution)/shard_map/all_to_all | solution.py:79
  296.8 100.7 %copy-start.5 = (s32[512]{0:T(512)S(1)}, s32[512]{0:T(512)}, u32[]{:S(2)}) copy-start(s32[512]{0:T(512)} %param.12) | copy-start | bytes 6148
  296.8 100.7 %copy-start.4 = (f32[512]{0:T(512)S(1)}, f32[512]{0:T(512)}, u32[]{:S(2)}) copy-start(f32[512]{0:T(512)} %param.13) | copy-start | bytes 6148
  298.0 143.4 %all-to-all-start.1 = ((f32[40,2,16,128]{3,1,0,2:T(2,128)}), f32[40,2,16,128]{3,1,0,2:T(2,128)S(1)}, u32[]{:S(2)}, u32[]{:S(2)}) async-start(f32[40,2,16,128]{3,1,0,2:T(2,128)} %copy.32), calls=%async_computation.1 | async-start | bytes 1310720 | tf_op jit(solution)/shard_map/all_to_all | solution.py:82
  441.3 0.8 copy-start.2
  444.4 13.5 %copy-start.3 = (f32[64,128]{1,0:T(8,128)S(1)}, f32[64,128]{1,0:T(8,128)}, u32[]{:S(2)}) copy-start(f32[64,128]{1,0:T(8,128)} %param.10) | copy-start | bytes 98308
  444.5 16.0 %copy-start.6 = (f32[128]{0:T(128)S(1)}, f32[128]{0:T(128)}, u32[]{:S(2)}) copy-start(f32[128]{0:T(128)} %param.11) | copy-start | bytes 1540
where the time goes:
time: 478 us; the launch traced here: 469 us
  waiting for transfers between devices  232 us (49%)
  other arithmetic  109 us (23%)
  starting transfers between devices  63.4 us (13%)
  matrix products  35.2 us (7%)
  local copies, waits for them, and re-layouts  28.1 us (6%)
    all_to_all x1, waiting for transfers between devices, on_device(): lax.all_to_all(scaled, 'spec', split_axis=0, concat_axis=2, tiled=True)  232 us
    all_to_all x1, starting transfers between devices, on_device(): lax.all_to_all(fourier, 'spec', split_axis=2, concat_axis=0, tiled=True)  55.9 us
    mul x1, other arithmetic, fourier_lookup(): -weights * jnp.sin(angles)  43.8 us
    mul x1, other arithmetic, fourier_lookup(): weights * jnp.cos(angles)  43.5 us
    all_to_all x2, local copies, waits for them, and re-layouts, on_device(): lax.all_to_all(scaled, 'spec', split_axis=0, concat_axis=2, tiled=True)  23 us
    mul x1, other arithmetic, prior_scale(): return shard.astype(jnp.float32) * spread[..., None]  16.7 us
    dot_general x1, matrix products, legendre_rows(): jnp.einsum('mpsj,mpsc->mpjc', legendre, spectral, precision=PRECISE)  13.6 us
    dot_general x1, matrix products, synthesize_row(): fields = jnp.einsum('kmq,mhqc->hkc', lookup, split_parts, precision=PRECISE)  13.5 us
  transfers between devices with their start and end apart: 2, of which 1 were waited for; matrix products, arithmetic and copies ran while one was open for 19% of the time, Pallas kernels for 0%

commit v1 on v0

v1 whole, which is shorter than its diff:
```python
import math

import jax
import jax.numpy as jnp
from jax import lax
from jax.experimental import pallas as pl
from jax.experimental.pallas import tpu as pltpu
from jax.sharding import PartitionSpec as P

NLON = 1280
FINE = 128

PRECISE = lax.Precision.HIGHEST
F32 = jnp.float32
BF16 = jnp.bfloat16


def prior_spread(orders, slots, waves):
    parity = jnp.arange(2, dtype=jnp.int32)[None, :, None]
    degree = orders[:, None, None] + 2 * slots[None, None, :] + parity
    spread = lax.rsqrt((degree + 1).astype(F32) * waves)
    return jnp.where(degree < waves, spread, jnp.zeros_like(spread))


def channel_kernel(peak_level, width, levels):
    height = jnp.arange(levels, dtype=F32)[:, None]
    offsets = (height - peak_level.astype(F32)[None, :]) / width[None, :]
    weights = jnp.exp(-offsets * offsets)
    return weights / jnp.sum(weights, axis=0, keepdims=True)


def split(x):
    high = x.astype(BF16)
    return high, (x - high.astype(F32)).astype(BF16)


def dot(a, b):
    return jnp.dot(a, b, preferred_element_type=F32)


def dot3(a, b):
    ah, al = split(a)
    bh, bl = split(b)
    return dot(ah, bh) + dot(al, bh) + dot(ah, bl)


def partial_kernel(pairs, padded, coef_ref, leg_ref, out_ref, pad_ref):
    waves, parities, slots, columns = coef_ref.shape
    groups = leg_ref.shape[0]
    per = pairs // 2
    lanes = leg_ref.shape[2]
    rows = lanes // pairs
    pad_ref[...] = jnp.zeros_like(pad_ref)
    owner = lax.broadcasted_iota(jnp.int32, (pairs, padded, lanes), 0)
    lane = lax.broadcasted_iota(jnp.int32, (pairs, padded, lanes), 2)
    keep = (lane % pairs == owner).reshape(pairs * padded, lanes)

    for g in range(groups):
        for i in range(pairs):
            pad_ref[g, i, pl.ds(0, slots), :] = coef_ref[g * per + i // 2, i % 2].astype(F32)
        values = pad_ref[g].reshape(pairs * padded, columns).astype(BF16)
        legs = leg_ref[g]
        if padded > slots:
            legs = jnp.concatenate((legs, jnp.zeros((padded - slots, lanes), F32)), axis=0)
        tiled = jnp.where(keep, jnp.concatenate([legs] * pairs, axis=0), 0.0)
        high, low = split(tiled)
        both = jnp.concatenate((high, low), axis=1)
        sums = lax.dot_general(both, values, (((0,), (0,)), ((), ())), preferred_element_type=F32)
        sums = sums[:lanes] + sums[lanes:]
        out_ref[:, pl.ds(g * pairs, pairs), :] = sums.reshape(rows, pairs, columns)


def partial_sums(coefficients, legs, pairs):
    waves, parities, slots, columns = coefficients.shape
    groups, _, lanes = legs.shape
    rows = lanes // pairs
    per = pairs // 2
    block = next(b for b in (8, 5, 4, 2, 1) if groups % b == 0)
    padded = -(-slots // 8) * 8
    if (pairs * padded) % 16:
        padded += 8

    def body(*refs):
        partial_kernel(pairs, padded, *refs)

    return pl.pallas_call(
        body,
        out_shape=jax.ShapeDtypeStruct((rows, groups * pairs, columns), F32),
        grid=(groups // block,),
        in_specs=[
            pl.BlockSpec((block * per, parities, slots, columns), lambda i: (i, 0, 0, 0)),
            pl.BlockSpec((block, slots, lanes), lambda i: (i, 0, 0)),
        ],
        out_specs=pl.BlockSpec((rows, block * pairs, columns), lambda i: (0, i, 0)),
        scratch_shapes=[pltpu.VMEM((block, pairs, padded, columns), F32)],
        name="partial_sums",
    )(coefficients, legs)


def row_kernel(
    count_ref, spectra_ref, fcos_ref, fsin_ref, ccos_ref, csin_ref, wide_ref, absorb_ref, resp_ref, out_ref,
    high_ref, low_ref, rhigh_ref, rlow_ref,
):
    step = pl.program_id(0)
    waves = fcos_ref.shape[1]
    levels = absorb_ref.shape[1]
    points = fcos_ref.shape[0]

    @pl.when(step == 0)
    def _():
        even = spectra_ref[pl.ds(0, waves, stride=2), :]
        odd = spectra_ref[pl.ds(1, waves, stride=2), :]
        half = even.shape[1] // 2
        real = jnp.concatenate((even[:, :half], odd[:, :half]), axis=1)
        imag = jnp.concatenate((even[:, half:], odd[:, half:]), axis=1)
        wide = wide_ref[...]
        for index, piece in enumerate((real, imag)):
            high, low = split(dot3(piece, wide))
            high_ref[pl.ds(index * waves, waves), :] = high
            low_ref[pl.ds(index * waves, waves), :] = low
        high, low = split(resp_ref[...])
        rhigh_ref[pl.ds(0, levels), :] = high
        rhigh_ref[pl.ds(levels, levels), :] = high
        rlow_ref[...] = low

    base_c = ccos_ref[pl.ds(step, 1), :]
    base_s = csin_ref[pl.ds(step, 1), :]
    fine_c = fcos_ref[...]
    fine_s = fsin_ref[...]
    cosine = base_c * fine_c - base_s * fine_s
    sine = -(base_s * fine_c + base_c * fine_s)
    lookup_high, lookup_low = split(jnp.concatenate((cosine, sine), axis=1))
    high = high_ref[...]
    temps = dot(lookup_high, high) + dot(lookup_low, high) + dot(lookup_high, low_ref[...])
    temps = jnp.concatenate((temps[:, :levels], temps[:, levels:]), axis=0)

    source = jnp.exp(0.5 * temps)
    layers = absorb_ref[...] * source
    before = lax.broadcasted_iota(jnp.int32, (2 * levels, levels), 0) % levels
    after = lax.broadcasted_iota(jnp.int32, (2 * levels, levels), 1)
    upper = jnp.where(before < after, 1.0, 0.0).astype(BF16)
    layers_high, layers_low = split(layers)
    above = dot(jnp.concatenate((layers_high, layers_low), axis=1), upper)
    emitted = source * jnp.exp(-above) * (1.0 - jnp.exp(-layers))
    place = step * points + lax.broadcasted_iota(jnp.int32, (2 * points, levels), 0) % points
    emitted = jnp.where(place < count_ref[0], emitted, 0.0)
    emitted_high, emitted_low = split(emitted)
    bright = dot(jnp.concatenate((emitted_high, emitted_low), axis=1), rhigh_ref[...])
    bright = bright + dot(emitted_high, rlow_ref[...])
    out_ref[0, 0] = bright[:points]
    out_ref[0, 1] = bright[points:]


def row_tables(row_count, waves, points):
    orders = jnp.arange(waves, dtype=jnp.int32)

    def angles(places):
        phases = places[:, None] * orders[None, :] % row_count
        return 2.0 * math.pi * phases.astype(F32) / row_count.astype(F32)

    fine = angles(jnp.arange(FINE, dtype=jnp.int32))
    coarse = angles(FINE * jnp.arange(points // FINE, dtype=jnp.int32))
    weights = jnp.where(orders == 0, 1.0, 2.0) * (2 * orders < row_count).astype(F32)
    return jnp.cos(fine), jnp.sin(fine), weights * jnp.cos(coarse), weights * jnp.sin(coarse)


def synthesize_row(spectra, row_counts, basis, absorb, kernel, points):
    waves = spectra.shape[0] // 2
    levels, channels = kernel.shape
    columns = spectra.shape[1]
    fcos, fsin, ccos, csin = row_tables(row_counts[0], waves, points)
    top = jnp.concatenate((basis, basis), axis=1)
    wide = jnp.concatenate((top, jnp.concatenate((basis, -basis), axis=1)), axis=0)
    steps = points // FINE

    def whole(*shape):
        return pl.BlockSpec(shape, lambda i, *_: (0,) * len(shape))

    return pl.pallas_call(
        row_kernel,
        out_shape=jax.ShapeDtypeStruct((1, 2, points, channels), F32),
        grid_spec=pltpu.PrefetchScalarGridSpec(
            num_scalar_prefetch=1,
            grid=(steps,),
            in_specs=[
                whole(2 * waves, columns),
                whole(FINE, waves),
                whole(FINE, waves),
                whole(steps, waves),
                whole(steps, waves),
                whole(*wide.shape),
                whole(1, levels),
                whole(levels, channels),
            ],
            out_specs=pl.BlockSpec((1, 2, FINE, channels), lambda i, *_: (0, 0, i, 0)),
            scratch_shapes=[
                pltpu.VMEM((2 * waves, 2 * levels), BF16),
                pltpu.VMEM((2 * waves, 2 * levels), BF16),
                pltpu.VMEM((2 * levels, channels), BF16),
                pltpu.VMEM((levels, channels), BF16),
            ],
        ),
        name="row_synthesis",
    )(row_counts, spectra, fcos, fsin, ccos, csin, wide, absorb[None, :], kernel)


def moved_coefficients(coefficients, legendre):
    waves, _, slots, _ = coefficients.shape
    first = lax.axis_index("spec") * slots
    spread = prior_spread(jnp.arange(waves, dtype=jnp.int32), first + jnp.arange(slots, dtype=jnp.int32), waves)
    scaled = coefficients.astype(F32) * spread[..., None]
    spectral = lax.all_to_all(scaled, "spec", split_axis=0, concat_axis=2, tiled=True)
    sums = jnp.einsum("mpsj,mpsc->mpjc", legendre, spectral, precision=PRECISE)
    sums = lax.all_to_all(sums, "spec", split_axis=2, concat_axis=0, tiled=True)
    return sums.reshape(2 * waves, sums.shape[-1])


def moved_legendre(coefficients, legendre, pairs):
    waves, _, slots, columns = coefficients.shape
    own, _, every, rows = legendre.shape
    orders = lax.axis_index("spec") * own + jnp.arange(own, dtype=jnp.int32)
    spread = prior_spread(orders, jnp.arange(every, dtype=jnp.int32), waves)
    legs = (legendre * spread[..., None]).reshape(own * 2 // pairs, pairs // 2, 2, every, rows)
    legs = jnp.transpose(legs, (0, 3, 4, 1, 2)).reshape(own * 2 // pairs, every, rows * pairs)
    legs = lax.all_to_all(legs, "spec", split_axis=1, concat_axis=0, tiled=True)
    sums = partial_sums(coefficients, legs, pairs)
    sums = lax.psum_scatter(sums, "spec", scatter_dimension=0, tiled=True)
    return sums.reshape(2 * waves, columns)


def on_device(coefficients, legendre, row_counts, basis, absorb, peak_level, width):
    kernel = channel_kernel(peak_level, width, basis.shape[1])
    own, _, _, rows = legendre.shape
    pairs = 128 // rows
    if pairs % 8 == 0 and (2 * own) % pairs == 0:
        spectra = moved_legendre(coefficients, legendre, pairs)
    else:
        spectra = moved_coefficients(coefficients, legendre)
    return synthesize_row(spectra, row_counts, basis, absorb, kernel, NLON)


def solution(mesh):
    placed = (
        P("draws", None, "spec", None),
        P("spec", None, None, None),
        P("spec"),
        P(),
        P(),
        P(),
        P(),
    )
    return jax.shard_map(
        on_device,
        mesh=mesh,
        in_specs=placed,
        out_specs=P(("draws", "spec"), None, None, None),
        check_vma=False,
    )
```

time: 478 us -> 244 us (0.51); the launches traced: 469 us -> 243 us
  other arithmetic: 109 us -> 10 us
  waiting for transfers between devices: 232 us -> 162 us
  starting transfers between devices: 63.4 us -> 7.45 us
  matrix products: 35.2 us -> 0 us
  Pallas kernels: 0 us -> 33 us
  between operations: 1.08 us -> 14.1 us
  local copies, waits for them, and re-layouts: 28.1 us -> 16.1 us
    all_to_all x2 -> x1, waiting for transfers between devices: 232 us -> 42.9 us  [moved_legendre(): legs = lax.all_to_all(legs, 'spec', split_axis=1, concat_axis=0, tiled=True)]
    reduce_scatter x0 -> x1, waiting for transfers between devices: none -> 120 us  [moved_legendre(): sums = lax.psum_scatter(sums, 'spec', scatter_dimension=0, tiled=True)]
    mul x7 -> x5, other arithmetic: 107 us -> 3.13 us  [the longest x1 1.81 us: moved_legendre(): legendre * spread[..., None]]
    all_to_all x2 -> x1, starting transfers between devices: 63.4 us -> 7.41 us  [moved_legendre(): legs = lax.all_to_all(legs, 'spec', split_axis=1, concat_axis=0, tiled=True)]
    dot_general x5 -> x0, matrix products: 35.2 us -> none  [the longest x1 13.6 us: legendre_rows(): jnp.einsum('mpsj,mpsc->mpjc', legendre, spectral, precision=PRECISE)]
    pallas_call x0 -> x2, Pallas kernels: none -> 33 us  [the longest x1 18.7 us: partial_sums(): pl.pallas_call(body, out_shape=jax.ShapeDtypeStruct((rows, groups * pairs...]
    all_to_all x2 -> x1, local copies, waits for them, and re-layouts: 23 us -> 1.8 us  [moved_legendre(): legs = lax.all_to_all(legs, 'spec', split_axis=1, concat_axis=0, tiled=True)]
    reshape x0 -> x3, local copies, waits for them, and re-layouts: none -> 7.09 us  [the longest x2 6.07 us: moved_legendre(): jnp.transpose(legs, (0, 3, 4, 1, 2))]
  transfers between devices with their start and end apart: 2 -> 2, of which waited for: 1 -> 2; matrix products, arithmetic and copies ran while one was open for 19% -> 6% of each run, Pallas kernels for 0% -> 0%
where the time goes in v1:
time: 244 us; the launch traced here: 243 us
  waiting for transfers between devices  162 us (66%)
  Pallas kernels  33 us (14%)
  local copies, waits for them, and re-layouts  16.1 us (7%)
  between operations  14.1 us (6%)
  other arithmetic  10 us (4%)
  starting transfers between devices  7.45 us (3%)
    reduce_scatter x1, waiting for transfers between devices, moved_legendre(): sums = lax.psum_scatter(sums, 'spec', scatter_dimension=0, tiled=True)  120 us
    all_to_all x1, waiting for transfers between devices, moved_legendre(): legs = lax.all_to_all(legs, 'spec', split_axis=1, concat_axis=0, tiled=True)  42.9 us
    pallas_call x1, Pallas kernels, partial_sums(): pl.pallas_call(body, out_shape=jax.ShapeDtypeStruct((rows, groups * pairs...  18.7 us
    pallas_call x1, Pallas kernels, synthesize_row(): pl.pallas_call(row_kernel, out_shape=jax.ShapeDtypeStruct((1, 2, points,...  14.3 us
    all_to_all x1, starting transfers between devices, moved_legendre(): legs = lax.all_to_all(legs, 'spec', split_axis=1, concat_axis=0, tiled=True)  7.41 us
    unnamed x7, local copies, waits for them, and re-layouts  7.22 us
    reshape x2, local copies, waits for them, and re-layouts, moved_legendre(): jnp.transpose(legs, (0, 3, 4, 1, 2))  6.07 us
    sin x1, other arithmetic, row_tables(): jnp.sin(fine)  5.14 us
  transfers between devices with their start and end apart: 2, of which 2 were waited for; matrix products, arithmetic and copies ran while one was open for 6% of the time, Pallas kernels for 0%

profile of v1, /device:TPU:0, one launch (start us, length us, event | category | flops | bytes accessed | tf_op | source)
XLA Modules:
  0.0 243.2 jit_solution(1296588129145655826)
XLA Ops:
  6.5 0.1 broadcast_add_fusion
  6.6 0.1 compare_select_fusion
  6.7 1.8 broadcast_multiply_fusion
  8.6 1.0 copy.21
  9.6 2.6 %reshape.74 = f32[10,320,128]{1,2,0:T(8,128)} reshape(f32[10,320,16,4,2]{1,4,3,2,0:T(2,128)S(1)} %bitcast.21) | data formatting | bytes 3276800 | tf_op jit(solution)/shard_map/reshape | solution.py:224
  12.2 3.4 %copy.14 = f32[10,320,128]{2,0,1:T(8,128)} copy(f32[10,320,128]{1,2,0:T(8,128)} %reshape.74) | data formatting | bytes 3276800 | tf_op jit(solution)/shard_map/reshape | solution.py:224
  15.7 7.4 %all-to-all-start = ((f32[10,320,128]{2,0,1:T(8,128)}), f32[10,320,128]{2,0,1:T(8,128)S(1)}, u32[]{:S(2)}, u32[]{:S(2)}) async-start(f32[10,320,128]{2,0,1:T(8,128)} %copy.14), calls=%async_computation | async-start | bytes 5242880 | tf_op jit(solution)/shard_map/all_to_all | solution.py:225
  23.1 0.0 reduce-scatter.2.cloned.1.call-start
  23.1 7.2 %copy.17.refs_0_ = bf16[640,2,20,128]{3,2,1,0:T(8,128)(2,1)} copy(bf16[640,2,20,128]{3,1,2,0:T(2,128)(2,1)} %param.7) | data formatting | bytes 13107200 | tf_op args[0]
  30.3 42.9 %all-to-all-done = f32[10,320,128]{2,0,1:T(8,128)S(1)} async-done(((f32[10,320,128]{2,0,1:T(8,128)}), f32[10,320,128]{2,0,1:T(8,128)S(1)}, u32[]{:S(2)}, u32[]{:S(2)}) %all-to-all-start) | async-done | bytes 1638432 | tf_op jit(solution)/shard_map/all_to_all | solution.py:225
  73.2 1.8 copy.16
  75.0 18.7 %partial_sums.1 = f32[16,1280,128]{2,1,0:T(8,128)} custom-call(bf16[640,2,20,128]{3,2,1,0:T(8,128)(2,1)} %copy.17.refs_0_, f32[160,20,128]{2,1,0:T(8,128)} %bitcast.19), custom_call_target="tpu_custom_call" | custom-call | tf_op jit(solution)/shard_map/partial_sums/pallas_call | solution.py:86
  93.7 0.0 copy-start
  93.7 0.0 copy-start.2
  93.7 0.0 copy-start.1
  93.7 0.0 reduce-scatter.2.cloned.1.call-update
  94.4 0.1 copy-done
  94.5 0.0 copy-done.2
  94.5 0.7 maximum_maximum_fusion.wide_ref
  95.2 5.1 %fusion.10 = (f32[128,640]{1,0:T(8,128)}, f32[128,640]{1,0:T(8,128)}) fusion(f32[]{:T(128)S(6)} %convert_element_type.23, pred[]{:T(512)S(6)} %lt.37, s32[]{:T(128)S(6)} %select_n.32), kind=kLoop, calls=%fused_computation.16 | loop fusion | flops 901120 | bytes 655369 | tf_op jit(solution)/shard_map/sin | solution.py:164
  100.3 0.0 copy-done.1
  100.3 0.1 fusion.9
  100.4 1.3 sine_multiply_fusion
  101.7 0.8 fusion.8.resp_ref
  102.5 119.6 %reduce-scatter.2.cloned.1.call-done = f32[1,1280,128]{2,1,0:T(8,128)} async-done(((f32[16,1280,128]{2,1,0:T(8,128)}), f32[1,1280,128]{2,1,0:T(8,128)}) %reduce-scatter.2.cloned.1.call-update) | async-done | bytes 655376 | tf_op jit(solution)/shard_map/reduce_scatter | solution.py:227
  222.0 14.3 %row_synthesis.1 = f32[1,2,1280,512]{3,2,1,0:T(8,128)} custom-call(s32[1]{0:T(128)} %copy.22.count_ref, f32[1280,128]{1,0:T(8,128)} %bitcast.22, f32[128,640]{1,0:T(8,128)} %get-tuple-element.8.fcos_ref, f32[128,640]{1,0:T(8,128)} %get-tuple-element.7.fsin_ref, f32[10,640]{1,0:T(8,128)} %get-tuple-element.6.ccos_ref, f32[10,640]{1,0:T(8,128)} %get-tuple-element.5.csin_ref, ...), custom_call_target="tpu_custom_call" | custom-call | tf_op jit(solution)/shard_map/row_synthesis/pallas_call | solution.py:179
  (6 shorter events, 0.0 us)
Async XLA Ops:
  15.7 57.5 %all-to-all-start = ((f32[10,320,128]{2,0,1:T(8,128)}), f32[10,320,128]{2,0,1:T(8,128)S(1)}, u32[]{:S(2)}, u32[]{:S(2)}) async-start(f32[10,320,128]{2,0,1:T(8,128)} %copy.14), calls=%async_computation | async-start | bytes 5242880 | tf_op jit(solution)/shard_map/all_to_all | solution.py:225
  23.1 199.0 %reduce-scatter.2.cloned.1.call-start = ((), (), s32[]{:S(2)}) async-start(), calls=%async_computation.2 | async-start | bytes 11141120 | tf_op jit(solution)/shard_map/reduce_scatter | solution.py:227
  93.7 0.8 copy-start
  93.7 0.8 copy-start.2
  93.7 6.6 %copy-start.1 = (f32[512]{0:T(512)S(1)}, f32[512]{0:T(512)}, u32[]{:S(2)}) copy-start(f32[512]{0:T(512)} %param.13) | copy-start | bytes 6148
Sparse Core Ops, SparseCore 0:
  93.9 128.1 reduce-scatter.1

commit v2 on v1

--- a/solution.py
+++ b/solution.py
@@ -44,57 +44,281 @@
     return dot(ah, bh) + dot(al, bh) + dot(ah, bl)
 
 
-def partial_kernel(pairs, padded, coef_ref, leg_ref, out_ref, pad_ref):
-    waves, parities, slots, columns = coef_ref.shape
-    groups = leg_ref.shape[0]
+def place_in_ring(n):
+    me = lax.axis_index("spec")
+    core = me % 2
+    side = (me // 2) % 2
+    layer = me // 4
+    return me, core, side, layer
+
+
+def exchange_kernel(
+    n, waves, coef_ref, leg_ref, out_ref, send_ref, legs_ref, wide_ref, sums_ref, near_ref, side_ref, far_ref,
+    leg_send, leg_recv, near_send, near_recv, side_send, side_recv, far_send, far_recv,
+):
+    me, core, side, layer = place_in_ring(n)
+    layers = n // 4
+    chunks = n // 2
+    chip = me // 2
+    rows = n
+    columns = coef_ref.shape[1]
+    every = leg_ref.shape[1]
+    slots = every // n
+    lanes = 128
+    pairs = lanes // rows
     per = pairs // 2
-    lanes = leg_ref.shape[2]
-    rows = lanes // pairs
-    pad_ref[...] = jnp.zeros_like(pad_ref)
-    owner = lax.broadcasted_iota(jnp.int32, (pairs, padded, lanes), 0)
-    lane = lax.broadcasted_iota(jnp.int32, (pairs, padded, lanes), 2)
-    keep = (lane % pairs == owner).reshape(pairs * padded, lanes)
-
-    for g in range(groups):
-        for i in range(pairs):
-            pad_ref[g, i, pl.ds(0, slots), :] = coef_ref[g * per + i // 2, i % 2].astype(F32)
-        values = pad_ref[g].reshape(pairs * padded, columns).astype(BF16)
-        legs = leg_ref[g]
-        if padded > slots:
-            legs = jnp.concatenate((legs, jnp.zeros((padded - slots, lanes), F32)), axis=0)
-        tiled = jnp.where(keep, jnp.concatenate([legs] * pairs, axis=0), 0.0)
-        high, low = split(tiled)
-        both = jnp.concatenate((high, low), axis=1)
-        sums = lax.dot_general(both, values, (((0,), (0,)), ((), ())), preferred_element_type=F32)
-        sums = sums[:lanes] + sums[lanes:]
-        out_ref[:, pl.ds(g * pairs, pairs), :] = sums.reshape(rows, pairs, columns)
-
-
-def partial_sums(coefficients, legs, pairs):
-    waves, parities, slots, columns = coefficients.shape
-    groups, _, lanes = legs.shape
-    rows = lanes // pairs
-    per = pairs // 2
-    block = next(b for b in (8, 5, 4, 2, 1) if groups % b == 0)
-    padded = -(-slots // 8) * 8
-    if (pairs * padded) % 16:
-        padded += 8
+    own = waves // n
+    groups = own // per
+    depth = per * slots * 2
+    part = groups * pairs
+    partner = me + 1 - 2 * core
+    across = me + 2 - 4 * side
+
+    def spot(z, y, c):
+        return (z * 2 + y) * 2 + c
+
+    def remote(src, dst, send_sem, recv_sem, target):
+        return pltpu.make_async_remote_copy(
+            src_ref=src, dst_ref=dst, send_sem=send_sem, recv_sem=recv_sem,
+            device_id={"spec": target}, device_id_type=pl.DeviceIdType.MESH,
+        )
+
+    def leg_copy(source, target):
+        return remote(send_ref.at[target], legs_ref.at[source], leg_send.at[target], leg_recv.at[source], target)
+
+    def near_copy(q):
+        return remote(sums_ref.at[q, 1 - core], near_ref.at[q], near_send.at[q], near_recv.at[q], partner)
+
+    def side_copy(q):
+        return remote(sums_ref.at[q, core, 1 - side], side_ref.at[q], side_send.at[q], side_recv.at[q], across)
+
+    def far_copy(q, source, target):
+        return remote(
+            sums_ref.at[q, core, side, target], far_ref.at[source, q],
+            far_send.at[target, q], far_recv.at[source, q], spot(target, side, core),
+        )
+
+    others = [(dz, dy, dc) for dz in range(layers) for dy in range(2) for dc in range(2)][1:]
+
+    def other(offset):
+        dz, dy, dc = offset
+        return spot((layer + dz) % layers, (side + dy) % 2, (core + dc) % 2)
+
+    barrier = pltpu.get_barrier_semaphore()
+    for offset in others:
+        pl.semaphore_signal(barrier, inc=1, device_id={"spec": other(offset)}, device_id_type=pl.DeviceIdType.MESH)
+
+    row = lax.broadcasted_iota(jnp.int32, (lanes, lanes), 0)
+    lane = lax.broadcasted_iota(jnp.int32, (lanes, lanes), 1)
+    row_at = row % rows
+    ordered = ((row_at % 2) * 2 + (row_at // 2) % 2) * layers + row_at // 4
+    moves = jnp.where(ordered * pairs + row // rows == lane, 1.0, 0.0)
+    leg_row = lax.broadcasted_iota(jnp.int32, (lanes, every), 0) // rows
+    leg_slot = lax.broadcasted_iota(jnp.int32, (lanes, every), 1)
+    degree_part = leg_row // 2 + leg_row % 2 + 2 * leg_slot
+
+    @pl.loop(0, groups // 2)
+    def _(double):
+        turned = []
+        for half in range(2):
+            g = double * 2 + half
+            degree = degree_part + (me * own + g * per)
+            spread = lax.rsqrt((degree + 1).astype(F32) * float(waves))
+            spread = jnp.where(degree < waves, spread, 0.0)
+            values = leg_ref[pl.ds(pl.multiple_of(g * lanes, lanes), lanes), :] * spread
+            turned.append(
+                lax.dot_general(
+                    values, moves, (((0,), (0,)), ((), ())), precision=PRECISE, preferred_element_type=F32
+                )
+            )
+        for k in range(n):
+            piece = [t[k * slots:(k + 1) * slots] for t in turned]
+            send_ref[k, pl.ds(pl.multiple_of(double * 2 * slots, 2 * slots), 2 * slots), :] = jnp.concatenate(piece, 0)
+
+    pl.semaphore_wait(barrier, len(others))
+    for offset in others:
+        target = other(offset)
+
+        @pl.when(me + target < n)
+        def _():
+            leg_copy(me, target).start()
+
+    legs_ref[me] = send_ref[me]
+
+    expand_row = lax.broadcasted_iota(jnp.int32, (depth, lanes), 0)
+    expand_lane = lax.broadcasted_iota(jnp.int32, (depth, lanes), 1) % pairs
+    keep = (expand_row // (2 * slots)) * 2 + expand_row % 2 == expand_lane
+
+    def partial(q, which):
+        owner = 2 * q + which
+
+        @pl.when(me + owner < n)
+        def _():
+            @pl.when(owner != me)
+            def _():
+                leg_copy(owner, me).wait_recv()
+
+            @pl.loop(0, groups // 2)
+            def _(double):
+                legs = legs_ref[owner, pl.ds(pl.multiple_of(double * 2 * slots, 2 * slots), 2 * slots), :]
+                wide_ref[pl.ds(0, 2 * slots, stride=2), :] = legs
+                wide_ref[pl.ds(1, 2 * slots, stride=2), :] = legs
+                for half in range(2):
+                    g = owner * groups + double * 2 + half
+                    values = coef_ref[pl.ds(pl.multiple_of(g * depth, depth), depth), :]
+                    one = wide_ref[pl.ds(half * 2 * slots, 2 * slots), :]
+                    tiled = jnp.where(keep, jnp.concatenate([one] * per, axis=0), 0.0)
+                    both = jnp.concatenate(split(tiled), axis=1)
+                    sums = lax.dot_general(both, values, (((0,), (0,)), ((), ())), preferred_element_type=F32)
+                    sums = (sums[:lanes] + sums[lanes:]).reshape(2, 2, layers, pairs, columns)
+                    at = pl.multiple_of(which * part + (double * 2 + half) * pairs, pairs)
+                    sums_ref[q, :, :, :, pl.ds(at, pairs), :] = sums
+
+        @pl.when(me + owner >= n)
+        def _():
+            sums_ref[q, :, :, :, pl.ds(which * part, part), :] = jnp.zeros((2, 2, layers, part, columns), F32)
+
+    def compute(q):
+        @pl.when(q + chip < chunks)
+        def _():
+            partial(q, 0)
+            partial(q, 1)
+            near_copy(q).start()
+
+    def merge_near(q):
+        @pl.when(q + chip < chunks)
+        def _():
+            near_copy(q).wait_recv()
+
+            for y in (0, 1):
+                @pl.loop(0, layers)
+                def _(z):
+                    sums_ref[q, core, y, z] += near_ref[q, y, z]
+
+            side_copy(q).start()
+
+    def merge_side(q):
+        here = q + chip < chunks
+        there = q + across // 2 < chunks
+
+        @pl.when(there)
+        def _():
+            side_copy(q).wait_recv()
+
+        @pl.when(jnp.logical_and(here, there))
+        def _():
+            @pl.loop(0, layers)
+            def _(z):
+                sums_ref[q, core, side, z] += side_ref[q, z]
+
+        @pl.when(jnp.logical_and(jnp.logical_not(here), there))
+        def _():
+            @pl.loop(0, layers)
+            def _(z):
+                sums_ref[q, core, side, z] = side_ref[q, z]
+
+        @pl.when(jnp.logical_or(here, there))
+        def _():
+            for dz in range(1, layers):
+                far_copy(q, layer, (layer + dz) % layers).start()
+
+    lag = min(5, chunks)
+
+    @pl.loop(0, chunks + 1)
+    def _(t):
+        @pl.when(t < chunks)
+        def _():
+            compute(t)
+
+        @pl.when(t >= 1)
+        def _():
+            merge_near(t - 1)
+
+        @pl.when(t >= lag)
+        def _():
+            merge_side(t - lag)
+
+    @pl.loop(chunks + 1 - lag, chunks)
+    def _(q):
+        merge_side(q)
+
+    @pl.loop(0, chunks)
+    def _(q):
+        at = pl.ds(pl.multiple_of(q * 2 * part, 2 * part), 2 * part)
+
+        @pl.when(q + 2 * layer < chunks)
+        def _():
+            out_ref[at, :] = sums_ref[q, core, side, layer]
+
+        @pl.when(q + 2 * layer >= chunks)
+        def _():
+            out_ref[at, :] = jnp.zeros((2 * part, columns), F32)
+
+        for dz in range(1, layers):
+            source = (layer + dz) % layers
+
+            @pl.when(q + 2 * source < chunks)
+            def _():
+                far_copy(q, source, layer).wait_recv()
+                out_ref[at, :] += far_ref[source, q]
+
+    for offset in others:
+        target = other(offset)
+
+        @pl.when(me + target < n)
+        def _():
+            leg_copy(me, target).wait_send()
+
+    @pl.loop(0, chunks)
+    def _(q):
+        @pl.when(q + chip < chunks)
+        def _():
+            near_copy(q).wait_send()
+            side_copy(q).wait_send()
+
+        @pl.when(q + 2 * layer < chunks)
+        def _():
+            for dz in range(1, layers):
+                far_copy(q, layer, (layer + dz) % layers).wait_send()
+
+
+def exchanged_sums(coefficients, legendre, n):
+    waves, _, slots, columns = coefficients.shape
+    own, _, every, rows = legendre.shape
+    dense = jnp.transpose(coefficients, (0, 2, 1, 3)).reshape(waves * slots * 2, columns)
+    legs = jnp.transpose(legendre, (0, 1, 3, 2)).reshape(own * 2 * rows, every)
+    layers, chunks = n // 4, n // 2
+    pairs = 128 // rows
+    groups = own * 2 // pairs
+    width = 2 * groups * pairs
+    dma = pltpu.SemaphoreType.DMA
 
     def body(*refs):
-        partial_kernel(pairs, padded, *refs)
+        exchange_kernel(n, waves, *refs)
 
     return pl.pallas_call(
         body,
-        out_shape=jax.ShapeDtypeStruct((rows, groups * pairs, columns), F32),
-        grid=(groups // block,),
-        in_specs=[
-            pl.BlockSpec((block * per, parities, slots, columns), lambda i: (i, 0, 0, 0)),
-            pl.BlockSpec((block, slots, lanes), lambda i: (i, 0, 0)),
+        out_shape=jax.ShapeDtypeStruct((2 * waves, columns), F32),
+        in_specs=[pl.BlockSpec(memory_space=pltpu.VMEM)] * 2,
+        out_specs=pl.BlockSpec(memory_space=pltpu.VMEM),
+        scratch_shapes=[
+            pltpu.VMEM((n, groups * slots, 128), F32),
+            pltpu.VMEM((n, groups * slots, 128), F32),
+            pltpu.VMEM((4 * slots, 128), F32),
+            pltpu.VMEM((chunks, 2, 2, layers, width, columns), F32),
+            pltpu.VMEM((chunks, 2, layers, width, columns), F32),
+            pltpu.VMEM((chunks, layers, width, columns), F32),
+            pltpu.VMEM((layers, chunks, width, columns), F32),
+            dma((n,)), dma((n,)),
+            dma((chunks,)), dma((chunks,)),
+            dma((chunks,)), dma((chunks,)),
+            dma((layers, chunks)), dma((layers, chunks)),
         ],
-        out_specs=pl.BlockSpec((rows, block * pairs, columns), lambda i: (0, i, 0)),
-        scratch_shapes=[pltpu.VMEM((block, pairs, padded, columns), F32)],
-        name="partial_sums",
-    )(coefficients, legs)
+        compiler_params=pltpu.CompilerParams(
+            collective_id=0, has_side_effects=True, vmem_limit_bytes=58 * 1024 * 1024
+        ),
+        name="exchanged_sums",
+    )(dense, legs)
 
 
 def row_kernel(
@@ -215,25 +439,15 @@
     return sums.reshape(2 * waves, sums.shape[-1])
 
 
-def moved_legendre(coefficients, legendre, pairs):
-    waves, _, slots, columns = coefficients.shape
-    own, _, every, rows = legendre.shape
-    orders = lax.axis_index("spec") * own + jnp.arange(own, dtype=jnp.int32)
-    spread = prior_spread(orders, jnp.arange(every, dtype=jnp.int32), waves)
-    legs = (legendre * spread[..., None]).reshape(own * 2 // pairs, pairs // 2, 2, every, rows)
-    legs = jnp.transpose(legs, (0, 3, 4, 1, 2)).reshape(own * 2 // pairs, every, rows * pairs)
-    legs = lax.all_to_all(legs, "spec", split_axis=1, concat_axis=0, tiled=True)
-    sums = partial_sums(coefficients, legs, pairs)
-    sums = lax.psum_scatter(sums, "spec", scatter_dimension=0, tiled=True)
-    return sums.reshape(2 * waves, columns)
-
-
 def on_device(coefficients, legendre, row_counts, basis, absorb, peak_level, width):
     kernel = channel_kernel(peak_level, width, basis.shape[1])
-    own, _, _, rows = legendre.shape
-    pairs = 128 // rows
-    if pairs % 8 == 0 and (2 * own) % pairs == 0:
-        spectra = moved_legendre(coefficients, legendre, pairs)
+    own, _, every, rows = legendre.shape
+    waves, _, slots, columns = coefficients.shape
+    n = waves // own
+    fits = n == rows and n % 8 == 0 and 128 % n == 0 and every == n * slots and columns == 128
+    fits = fits and (128 // n) % 8 == 0 and own % (128 // n) == 0 and slots % 4 == 0
+    if fits and (slots * 128 // n) % 16 == 0 and 2 * waves >= 2 * slots * n:
+        spectra = exchanged_sums(coefficients, legendre, n)
     else:
         spectra = moved_coefficients(coefficients, legendre)
     return synthesize_row(spectra, row_counts, basis, absorb, kernel, NLON)

time: 244 us -> 123 us (0.50)
  waiting for transfers between devices: 162 us -> 0 us
  Pallas kernels: 33 us -> 110 us
  local copies, waits for them, and re-layouts: 16.1 us -> 0 us
  between operations: 14.1 us -> 0.68 us
  starting transfers between devices: 7.45 us -> 0 us
    reduce_scatter x1 -> x0, waiting for transfers between devices: 120 us -> none  [moved_legendre(): sums = lax.psum_scatter(sums, 'spec', scatter_dimension=0, tiled=True)]
    pallas_call x1, Pallas kernels: 18.7 us -> 95.8 us  [exchanged_sums(): pl.pallas_call(body, out_shape=jax.ShapeDtypeStruct((2 * waves, columns),...]
    all_to_all x1 -> x0, waiting for transfers between devices: 42.9 us -> none  [moved_legendre(): legs = lax.all_to_all(legs, 'spec', split_axis=1, concat_axis=0, tiled=True)]
    all_to_all x1 -> x0, starting transfers between devices: 7.41 us -> none  [moved_legendre(): legs = lax.all_to_all(legs, 'spec', split_axis=1, concat_axis=0, tiled=True)]
    unnamed x7 -> x0, local copies, waits for them, and re-layouts: 7.22 us -> none
    reshape x3 -> x0, local copies, waits for them, and re-layouts: 7.09 us -> none  [the longest x2 6.07 us: moved_legendre(): jnp.transpose(legs, (0, 3, 4, 1, 2))]
  transfers between devices with their start and end apart: 2 -> 0, of which waited for: 2 -> 0; matrix products, arithmetic and copies ran while one was open for 6% -> 0% of each run, Pallas kernels for 0% -> 0%
where the time goes in v2:
time: 123 us
  Pallas kernels  110 us (89%)
  other arithmetic  11.7 us (10%)
    pallas_call x1, Pallas kernels, exchanged_sums(): pl.pallas_call(body, out_shape=jax.ShapeDtypeStruct((2 * waves, columns),...  95.8 us
    pallas_call x1, Pallas kernels, synthesize_row(): pl.pallas_call(row_kernel, out_shape=jax.ShapeDtypeStruct((1, 2, points,...  14.3 us
    sin x1, other arithmetic, row_tables(): jnp.sin(fine)  5.16 us

profile of v2, /device:TPU:0, one launch (start us, length us, event | category | flops | bytes accessed | tf_op | source)
XLA Modules:
  0.0 122.5 jit_solution(14674338302429704129)
XLA Ops:
  0.7 0.7 convert_element_type.17
  1.4 0.8 fusion.9
  2.1 0.8 neg.6
  2.9 1.3 %sine_multiply_fusion = (f32[10,640]{1,0:T(8,128)}, f32[10,640]{1,0:T(8,128)}) fusion(f32[640]{0:T(1024)S(1)} %select_select_fusion, f32[]{:T(128)S(6)} %convert_element_type.15, pred[]{:T(512)S(6)} %lt.25, s32[]{:T(128)S(6)} %select_n.23, s32[10]{0:T(128)S(1)} %iota_multiply_fusion), kind=kLoop, calls=%fused_computation.20 | loop fusion | flops 83200 | bytes 53809 | tf_op jit(solution)/shard_map/mul | solution.py:388
  4.2 1.5 %maximum_maximum_fusion.wide_ref = f32[128,256]{1,0:T(8,128)} fusion(f32[64,128]{1,0:T(8,128)S(1)} %neg.6, f32[64,128]{1,0:T(8,128)} %param.10), kind=kLoop, calls=%fused_computation.15 | loop fusion | flops 98304 | bytes 196608 | tf_op jit(solution)/shard_map/concatenate | solution.py:397
  5.7 1.5 %fusion.8.resp_ref = f32[128,512]{1,0:T(8,128)} fusion(f32[512]{0:T(512)S(1)} %fusion.9, f32[512]{0:T(512)} %param.13, f32[512]{0:T(512)S(1)} %convert_element_type.17), kind=kLoop, calls=%fused_computation.11 | loop fusion | flops 327680 | bytes 268288 | tf_op jit(solution)/shard_map/div | solution.py:29
  7.2 5.2 %fusion.10 = (f32[128,640]{1,0:T(8,128)}, f32[128,640]{1,0:T(8,128)}) fusion(f32[]{:T(128)S(6)} %convert_element_type.15, pred[]{:T(512)S(6)} %lt.25, s32[]{:T(128)S(6)} %select_n.23), kind=kLoop, calls=%fused_computation.13 | loop fusion | flops 901120 | bytes 655369 | tf_op jit(solution)/shard_map/sin | solution.py:388
  12.4 95.8 %exchanged_sums.1.spectra_ref = f32[1280,128]{1,0:T(8,128)} custom-call(bf16[25600,128]{1,0:T(8,128)(2,1)} %bitcast.12, f32[1280,320]{1,0:T(8,128)} %bitcast.13), custom_call_target="tpu_custom_call" | custom-call | tf_op jit(solution)/shard_map/exchanged_sums/pallas_call | solution.py:299
  108.2 14.3 %row_synthesis.1 = f32[1,2,1280,512]{3,2,1,0:T(8,128)} custom-call(s32[1]{0:T(128)} %copy.8.count_ref, f32[1280,128]{1,0:T(8,128)} %exchanged_sums.1.spectra_ref, f32[128,640]{1,0:T(8,128)} %get-tuple-element.8.fcos_ref, f32[128,640]{1,0:T(8,128)} %get-tuple-element.7.fsin_ref, f32[10,640]{1,0:T(8,128)} %get-tuple-element.6.ccos_ref, ...), custom_call_target="tpu_custom_call" | custom-call | tf_op jit(solution)/shard_map/row_synthesis/pallas_call | solution.py:403
  (2 shorter events, 0.0 us)

commit v3 on v2

--- a/solution.py
+++ b/solution.py
@@ -1,3 +1,4 @@
+import functools
 import math
 
 import jax
@@ -22,13 +23,6 @@
     return jnp.where(degree < waves, spread, jnp.zeros_like(spread))
 
 
-def channel_kernel(peak_level, width, levels):
-    height = jnp.arange(levels, dtype=F32)[:, None]
-    offsets = (height - peak_level.astype(F32)[None, :]) / width[None, :]
-    weights = jnp.exp(-offsets * offsets)
-    return weights / jnp.sum(weights, axis=0, keepdims=True)
-
-
 def split(x):
     high = x.astype(BF16)
     return high, (x - high.astype(F32)).astype(BF16)
@@ -53,15 +47,16 @@
 
 
 def exchange_kernel(
-    n, waves, coef_ref, leg_ref, out_ref, send_ref, legs_ref, wide_ref, sums_ref, near_ref, side_ref, far_ref,
-    leg_send, leg_recv, near_send, near_recv, side_send, side_recv, far_send, far_recv,
+    n, draws, waves, coef_hbm, leg_ref, out_ref, coef_ref, send_ref, legs_ref, wide_ref, sums_ref, near_ref, side_ref,
+    far_ref, coef_sem, leg_send, leg_recv, pass_send, near_send, near_recv, side_send, side_recv, far_send, far_recv,
 ):
     me, core, side, layer = place_in_ring(n)
     layers = n // 4
-    chunks = n // 2
+    chunks = n
     chip = me // 2
+    draw = lax.axis_index("draws")
     rows = n
-    columns = coef_ref.shape[1]
+    columns = coef_hbm.shape[1]
     every = leg_ref.shape[1]
     slots = every // n
     lanes = 128
@@ -86,6 +81,13 @@
     def leg_copy(source, target):
         return remote(send_ref.at[target], legs_ref.at[source], leg_send.at[target], leg_recv.at[source], target)
 
+    def pass_copy(source):
+        return pltpu.make_async_remote_copy(
+            src_ref=legs_ref.at[source], dst_ref=legs_ref.at[source],
+            send_sem=pass_send.at[source], recv_sem=leg_recv.at[source],
+            device_id={"draws": 1 - draw}, device_id_type=pl.DeviceIdType.MESH,
+        )
+
     def near_copy(q):
         return remote(sums_ref.at[q, 1 - core], near_ref.at[q], near_send.at[q], near_recv.at[q], partner)
 
@@ -104,7 +106,12 @@
         dz, dy, dc = offset
         return spot((layer + dz) % layers, (side + dy) % 2, (core + dc) % 2)
 
+    coef_copy = pltpu.make_async_copy(coef_hbm, coef_ref, coef_sem)
+    coef_copy.start()
+    paired = draws == 2
     barrier = pltpu.get_barrier_semaphore()
+    if paired:
+        pl.semaphore_signal(barrier, inc=1, device_id={"draws": 1 - draw}, device_id_type=pl.DeviceIdType.MESH)
     for offset in others:
         pl.semaphore_signal(barrier, inc=1, device_id={"spec": other(offset)}, device_id_type=pl.DeviceIdType.MESH)
 
@@ -135,26 +142,42 @@
             piece = [t[k * slots:(k + 1) * slots] for t in turned]
             send_ref[k, pl.ds(pl.multiple_of(double * 2 * slots, 2 * slots), 2 * slots), :] = jnp.concatenate(piece, 0)
 
-    pl.semaphore_wait(barrier, len(others))
+    pl.semaphore_wait(barrier, len(others) + paired)
+    sends = (core == draw) if paired else (core >= 0)
     for offset in others:
         target = other(offset)
 
-        @pl.when(me + target < n)
+        @pl.when(jnp.logical_and(sends, me + target < n))
         def _():
             leg_copy(me, target).start()
 
     legs_ref[me] = send_ref[me]
+    coef_copy.wait()
+
+    def receive(owner):
+        wanted = jnp.logical_and(owner != me, me + owner < n)
+        if not paired:
+            return
+
+        @pl.when(jnp.logical_and(wanted, owner % 2 == draw))
+        def _():
+            leg_copy(owner, me).wait_recv()
+            pass_copy(owner).start()
 
     expand_row = lax.broadcasted_iota(jnp.int32, (depth, lanes), 0)
     expand_lane = lax.broadcasted_iota(jnp.int32, (depth, lanes), 1) % pairs
     keep = (expand_row // (2 * slots)) * 2 + expand_row % 2 == expand_lane
 
-    def partial(q, which):
-        owner = 2 * q + which
+    def partial(q):
+        owner = q
 
         @pl.when(me + owner < n)
         def _():
-            @pl.when(owner != me)
+            waits = owner != me
+            if paired:
+                waits = jnp.logical_and(waits, owner % 2 != draw)
+
+            @pl.when(waits)
             def _():
                 leg_copy(owner, me).wait_recv()
 
@@ -171,22 +194,21 @@
                     both = jnp.concatenate(split(tiled), axis=1)
                     sums = lax.dot_general(both, values, (((0,), (0,)), ((), ())), preferred_element_type=F32)
                     sums = (sums[:lanes] + sums[lanes:]).reshape(2, 2, layers, pairs, columns)
-                    at = pl.multiple_of(which * part + (double * 2 + half) * pairs, pairs)
+                    at = pl.multiple_of((double * 2 + half) * pairs, pairs)
                     sums_ref[q, :, :, :, pl.ds(at, pairs), :] = sums
 
         @pl.when(me + owner >= n)
         def _():
-            sums_ref[q, :, :, :, pl.ds(which * part, part), :] = jnp.zeros((2, 2, layers, part, columns), F32)
+            sums_ref[q] = jnp.zeros((2, 2, layers, part, columns), F32)
 
     def compute(q):
-        @pl.when(q + chip < chunks)
-        def _():
-            partial(q, 0)
-            partial(q, 1)
+        @pl.when(q + 2 * chip < chunks)
+        def _():
+            partial(q)
             near_copy(q).start()
 
     def merge_near(q):
-        @pl.when(q + chip < chunks)
+        @pl.when(q + 2 * chip < chunks)
         def _():
             near_copy(q).wait_recv()
 
@@ -198,8 +220,8 @@
             side_copy(q).start()
 
     def merge_side(q):
-        here = q + chip < chunks
-        there = q + across // 2 < chunks
+        here = q + 2 * chip < chunks
+        there = q + 2 * (across // 2) < chunks
 
         @pl.when(there)
         def _():
@@ -222,10 +244,17 @@
             for dz in range(1, layers):
                 far_copy(q, layer, (layer + dz) % layers).start()
 
-    lag = min(5, chunks)
+    lag = min(7, chunks)
+    ahead = 2
+    for owner in range(ahead):
+        receive(owner)
 
     @pl.loop(0, chunks + 1)
     def _(t):
+        @pl.when(t + ahead < chunks)
+        def _():
+            receive(t + ahead)
+
         @pl.when(t < chunks)
         def _():
             compute(t)
@@ -244,20 +273,20 @@
 
     @pl.loop(0, chunks)
     def _(q):
-        at = pl.ds(pl.multiple_of(q * 2 * part, 2 * part), 2 * part)
-
-        @pl.when(q + 2 * layer < chunks)
+        at = pl.ds(pl.multiple_of(q * part, part), part)
+
+        @pl.when(q + 4 * layer < chunks)
         def _():
             out_ref[at, :] = sums_ref[q, core, side, layer]
 
-        @pl.when(q + 2 * layer >= chunks)
-        def _():
-            out_ref[at, :] = jnp.zeros((2 * part, columns), F32)
+        @pl.when(q + 4 * layer >= chunks)
+        def _():
+            out_ref[at, :] = jnp.zeros((part, columns), F32)
 
         for dz in range(1, layers):
             source = (layer + dz) % layers
 
-            @pl.when(q + 2 * source < chunks)
+            @pl.when(q + 4 * source < chunks)
             def _():
                 far_copy(q, source, layer).wait_recv()
                 out_ref[at, :] += far_ref[source, q]
@@ -265,43 +294,51 @@
     for offset in others:
         target = other(offset)
 
-        @pl.when(me + target < n)
+        @pl.when(jnp.logical_and(sends, me + target < n))
         def _():
             leg_copy(me, target).wait_send()
+
+    if paired:
+        @pl.loop(0, n)
+        def _(owner):
+            @pl.when(jnp.logical_and(owner != me, jnp.logical_and(me + owner < n, owner % 2 == draw)))
+            def _():
+                pass_copy(owner).wait_send()
 
     @pl.loop(0, chunks)
     def _(q):
-        @pl.when(q + chip < chunks)
+        @pl.when(q + 2 * chip < chunks)
         def _():
             near_copy(q).wait_send()
             side_copy(q).wait_send()
 
-        @pl.when(q + 2 * layer < chunks)
+        @pl.when(q + 4 * layer < chunks)
         def _():
             for dz in range(1, layers):
                 far_copy(q, layer, (layer + dz) % layers).wait_send()
 
 
-def exchanged_sums(coefficients, legendre, n):
+def exchanged_sums(coefficients, legendre, n, draws):
     waves, _, slots, columns = coefficients.shape
     own, _, every, rows = legendre.shape
     dense = jnp.transpose(coefficients, (0, 2, 1, 3)).reshape(waves * slots * 2, columns)
     legs = jnp.transpose(legendre, (0, 1, 3, 2)).reshape(own * 2 * rows, every)
-    layers, chunks = n // 4, n // 2
+    layers, chunks = n // 4, n
     pairs = 128 // rows
     groups = own * 2 // pairs
-    width = 2 * groups * pairs
+    width = groups * pairs
     dma = pltpu.SemaphoreType.DMA
 
     def body(*refs):
-        exchange_kernel(n, waves, *refs)
+        exchange_kernel(n, draws, waves, *refs)
 
     return pl.pallas_call(
         body,
         out_shape=jax.ShapeDtypeStruct((2 * waves, columns), F32),
-        in_specs=[pl.BlockSpec(memory_space=pltpu.VMEM)] * 2,
+        in_specs=[pl.BlockSpec(memory_space=pl.ANY), pl.BlockSpec(memory_space=pltpu.VMEM)],
         out_specs=pl.BlockSpec(memory_space=pltpu.VMEM),
         scratch_shapes=[
+            pltpu.VMEM(dense.shape, BF16),
             pltpu.VMEM((n, groups * slots, 128), F32),
             pltpu.VMEM((n, groups * slots, 128), F32),
             pltpu.VMEM((4 * slots, 128), F32),
@@ -309,7 +346,7 @@
             pltpu.VMEM((chunks, 2, layers, width, columns), F32),
             pltpu.VMEM((chunks, layers, width, columns), F32),
             pltpu.VMEM((layers, chunks, width, columns), F32),
-            dma((n,)), dma((n,)),
+            dma, dma((n,)), dma((n,)), dma((n,)),
             dma((chunks,)), dma((chunks,)),
             dma((chunks,)), dma((chunks,)),
             dma((layers, chunks)), dma((layers, chunks)),
@@ -322,27 +359,53 @@
 
 
 def row_kernel(
-    count_ref, spectra_ref, fcos_ref, fsin_ref, ccos_ref, csin_ref, wide_ref, absorb_ref, resp_ref, out_ref,
-    high_ref, low_ref, rhigh_ref, rlow_ref,
+    count_ref, spectra_ref, basis_ref, absorb_ref, peak_ref, width_ref, out_ref,
+    fcos_ref, fsin_ref, ccos_ref, csin_ref, high_ref, low_ref, rhigh_ref, rlow_ref,
 ):
     step = pl.program_id(0)
     waves = fcos_ref.shape[1]
     levels = absorb_ref.shape[1]
     points = fcos_ref.shape[0]
+    tiny = 16
+    middle = points // tiny
 
     @pl.when(step == 0)
     def _():
+        count = count_ref[0].astype(F32)
+        table = (tiny + middle + ccos_ref.shape[0], waves)
+        index = lax.broadcasted_iota(jnp.int32, table, 0)
+        order = lax.broadcasted_iota(jnp.int32, table, 1)
+        places = jnp.where(index < tiny, index, (index - tiny) * tiny)
+        places = jnp.where(index < tiny + middle, places, (index - tiny - middle) * points)
+        phases = (places * order).astype(F32)
+        phases = phases - jnp.floor(phases / count) * count
+        angles = 2.0 * math.pi * phases / count
+        cosine, sine = jnp.cos(angles), jnp.sin(angles)
+        weights = jnp.where(order == 0, 1.0, 2.0) * jnp.where(2 * order < count_ref[0], 1.0, 0.0)
+        first = tiny + middle
+        ccos_ref[...] = (cosine * weights)[first:]
+        csin_ref[...] = (sine * weights)[first:]
+        for b in range(middle):
+            turn_c, turn_s = cosine[tiny + b:tiny + b + 1], sine[tiny + b:tiny + b + 1]
+            fcos_ref[pl.ds(b * tiny, tiny), :] = cosine[:tiny] * turn_c - sine[:tiny] * turn_s
+            fsin_ref[pl.ds(b * tiny, tiny), :] = sine[:tiny] * turn_c + cosine[:tiny] * turn_s
+
         even = spectra_ref[pl.ds(0, waves, stride=2), :]
         odd = spectra_ref[pl.ds(1, waves, stride=2), :]
         half = even.shape[1] // 2
         real = jnp.concatenate((even[:, :half], odd[:, :half]), axis=1)
         imag = jnp.concatenate((even[:, half:], odd[:, half:]), axis=1)
-        wide = wide_ref[...]
+        basis = basis_ref[...]
+        top = jnp.concatenate((basis, basis), axis=1)
+        wide = jnp.concatenate((top, jnp.concatenate((basis, -basis), axis=1)), axis=0)
         for index, piece in enumerate((real, imag)):
             high, low = split(dot3(piece, wide))
             high_ref[pl.ds(index * waves, waves), :] = high
             low_ref[pl.ds(index * waves, waves), :] = low
-        high, low = split(resp_ref[...])
+        height = lax.broadcasted_iota(jnp.int32, rlow_ref.shape, 0)
+        offsets = (height - peak_ref[...]).astype(F32) / width_ref[...]
+        shape = jnp.exp(-offsets * offsets)
+        high, low = split(shape / jnp.sum(shape, axis=0, keepdims=True))
         rhigh_ref[pl.ds(0, levels), :] = high
         rhigh_ref[pl.ds(levels, levels), :] = high
         rlow_ref[...] = low
@@ -375,27 +438,12 @@
     out_ref[0, 1] = bright[points:]
 
 
-def row_tables(row_count, waves, points):
-    orders = jnp.arange(waves, dtype=jnp.int32)
-
-    def angles(places):
-        phases = places[:, None] * orders[None, :] % row_count
-        return 2.0 * math.pi * phases.astype(F32) / row_count.astype(F32)
-
-    fine = angles(jnp.arange(FINE, dtype=jnp.int32))
-    coarse = angles(FINE * jnp.arange(points // FINE, dtype=jnp.int32))
-    weights = jnp.where(orders == 0, 1.0, 2.0) * (2 * orders < row_count).astype(F32)
-    return jnp.cos(fine), jnp.sin(fine), weights * jnp.cos(coarse), weights * jnp.sin(coarse)
-
-
-def synthesize_row(spectra, row_counts, basis, absorb, kernel, points):
+def synthesize_row(spectra, row_counts, basis, absorb, peak_level, width, points):
     waves = spectra.shape[0] // 2
-    levels, channels = kernel.shape
+    levels, channels = absorb.shape[0], width.shape[0]
     columns = spectra.shape[1]
-    fcos, fsin, ccos, csin = row_tables(row_counts[0], waves, points)
-    top = jnp.concatenate((basis, basis), axis=1)
-    wide = jnp.concatenate((top, jnp.concatenate((basis, -basis), axis=1)), axis=0)
     steps = points // FINE
+    coarse = -(-steps // 8) * 8
 
     def whole(*shape):
         return pl.BlockSpec(shape, lambda i, *_: (0,) * len(shape))
@@ -408,16 +456,17 @@
             grid=(steps,),
             in_specs=[
                 whole(2 * waves, columns),
-                whole(FINE, waves),
-                whole(FINE, waves),
-                whole(steps, waves),
-                whole(steps, waves),
-                whole(*wide.shape),
+                whole(*basis.shape),
                 whole(1, levels),
-                whole(levels, channels),
+                whole(1, channels),
+                whole(1, channels),
             ],
             out_specs=pl.BlockSpec((1, 2, FINE, channels), lambda i, *_: (0, 0, i, 0)),
             scratch_shapes=[
+                pltpu.VMEM((FINE, waves), F32),
+                pltpu.VMEM((FINE, waves), F32),
+                pltpu.VMEM((coarse, waves), F32),
+                pltpu.VMEM((coarse, waves), F32),
                 pltpu.VMEM((2 * waves, 2 * levels), BF16),
                 pltpu.VMEM((2 * waves, 2 * levels), BF16),
                 pltpu.VMEM((2 * levels, channels), BF16),
@@ -425,7 +474,7 @@
             ],
         ),
         name="row_synthesis",
-    )(row_counts, spectra, fcos, fsin, ccos, csin, wide, absorb[None, :], kernel)
+    )(row_counts, spectra, basis, absorb[None, :], peak_level[None, :], width[None, :])
 
 
 def moved_coefficients(coefficients, legendre):
@@ -439,18 +488,17 @@
     return sums.reshape(2 * waves, sums.shape[-1])
 
 
-def on_device(coefficients, legendre, row_counts, basis, absorb, peak_level, width):
-    kernel = channel_kernel(peak_level, width, basis.shape[1])
+def on_device(draws, coefficients, legendre, row_counts, basis, absorb, peak_level, width):
     own, _, every, rows = legendre.shape
     waves, _, slots, columns = coefficients.shape
     n = waves // own
     fits = n == rows and n % 8 == 0 and 128 % n == 0 and every == n * slots and columns == 128
     fits = fits and (128 // n) % 8 == 0 and own % (128 // n) == 0 and slots % 4 == 0
     if fits and (slots * 128 // n) % 16 == 0 and 2 * waves >= 2 * slots * n:
-        spectra = exchanged_sums(coefficients, legendre, n)
+        spectra = exchanged_sums(coefficients, legendre, n, draws)
     else:
         spectra = moved_coefficients(coefficients, legendre)
-    return synthesize_row(spectra, row_counts, basis, absorb, kernel, NLON)
+    return synthesize_row(spectra, row_counts, basis, absorb, peak_level, width, NLON)
 
 
 def solution(mesh):
@@ -464,7 +512,7 @@
         P(),
     )
     return jax.shard_map(
-        on_device,
+        functools.partial(on_device, mesh.shape["draws"]),
         mesh=mesh,
         in_specs=placed,
         out_specs=P(("draws", "spec"), None, None, None),

time: 123 us -> 99.4 us (0.81)
  Pallas kernels: 110 us -> 97.7 us
  other arithmetic: 11.7 us -> 0 us
    pallas_call x1, Pallas kernels: 95.8 us -> 83.3 us  [exchanged_sums(): pl.pallas_call(body, out_shape=jax.ShapeDtypeStruct((2 * waves, columns),...]
    sin x1 -> x0, other arithmetic: 5.16 us -> none  [row_tables(): jnp.sin(fine)]
    concatenate x1 -> x0, other arithmetic: 1.52 us -> none  [synthesize_row(): jnp.concatenate((top, jnp.concatenate((basis, -basis), axis=1)), axis=0)]
    div x1 -> x0, other arithmetic: 1.48 us -> none  [channel_kernel(): return weights / jnp.sum(weights, axis=0, keepdims=True)]
    mul x3 -> x0, other arithmetic: 1.31 us -> none  [the longest x1 1.3 us: row_tables(): weights * jnp.sin(coarse)]
where the time goes in v3:
time: 99.4 us; the launch traced here: 98.3 us
  Pallas kernels  97.7 us (98%)
    pallas_call x1, Pallas kernels, exchanged_sums(): pl.pallas_call(body, out_shape=jax.ShapeDtypeStruct((2 * waves, columns),...  83.3 us
    pallas_call x1, Pallas kernels, synthesize_row(): pl.pallas_call(row_kernel, out_shape=jax.ShapeDtypeStruct((1, 2, points,...  14.4 us

profile of v3, /device:TPU:0, one launch (start us, length us, event | category | flops | bytes accessed | tf_op | source)
XLA Modules:
  0.0 98.3 jit_solution(1552809850746203555)
XLA Ops:
  0.7 83.3 %exchanged_sums.1.spectra_ref = f32[1280,128]{1,0:T(8,128)} custom-call(bf16[25600,128]{1,0:T(8,128)(2,1)} %bitcast.9, f32[1280,320]{1,0:T(8,128)} %bitcast.10), custom_call_target="tpu_custom_call" | custom-call | tf_op jit(solution)/shard_map/exchanged_sums/pallas_call | solution.py:335
  83.9 14.4 %row_synthesis.1 = f32[1,2,1280,512]{3,2,1,0:T(8,128)} custom-call(s32[1]{0:T(128)S(6)} %copy.8.count_ref, f32[1280,128]{1,0:T(8,128)} %exchanged_sums.1.spectra_ref, f32[64,128]{1,0:T(8,128)} %basis_ref.1, f32[1,128]{1,0:T(1,128)} %bitcast.13, s32[1,512]{1,0:T(1,128)} %bitcast.11, f32[1,512]{1,0:T(1,128)} %bitcast.12), custom_call_target="tpu_custom_call" | custom-call | tf_op jit(solution)/shard_map/row_synthesis/pallas_call | solution.py:451

commit v4 on v3

--- a/solution.py
+++ b/solution.py
@@ -9,7 +9,8 @@
 from jax.sharding import PartitionSpec as P
 
 NLON = 1280
-FINE = 128
+FINE = 256
+BLOCK = 128
 
 PRECISE = lax.Precision.HIGHEST
 F32 = jnp.float32
@@ -47,8 +48,8 @@
 
 
 def exchange_kernel(
-    n, draws, waves, coef_hbm, leg_ref, out_ref, coef_ref, send_ref, legs_ref, wide_ref, sums_ref, near_ref, side_ref,
-    far_ref, coef_sem, leg_send, leg_recv, pass_send, near_send, near_recv, side_send, side_recv, far_send, far_recv,
+    n, draws, waves, count_ref, coef_hbm, leg_ref, basis_ref, out_ref, coef_ref, send_ref, legs_ref, wide_ref, sums_ref, near_ref, side_ref,
+    far_ref, held_ref, fcos_ref, fsin_ref, coef_sem, leg_send, leg_recv, pass_send, near_send, near_recv, side_send, side_recv, far_send, far_recv,
 ):
     me, core, side, layer = place_in_ring(n)
     layers = n // 4
@@ -244,12 +245,77 @@
             for dz in range(1, layers):
                 far_copy(q, layer, (layer + dz) % layers).start()
 
-    lag = min(7, chunks)
+    points = out_ref.shape[0]
+    tiny = 16
+    middle = BLOCK // tiny
+    both_waves = 2 * own
+    table = (tiny + middle + -(-points // BLOCK // 8) * 8, 2 * both_waves)
+    first = tiny + middle
+    out_ref[...] = jnp.zeros_like(out_ref)
+
+    def collect(q, which):
+        at = pl.ds(which * part, part)
+
+        @pl.when(q + 4 * layer < chunks)
+        def _():
+            held_ref[at, :] = sums_ref[q, core, side, layer]
+
+        @pl.when(q + 4 * layer >= chunks)
+        def _():
+            held_ref[at, :] = jnp.zeros((part, columns), F32)
+
+        for dz in range(1, layers):
+            source = (layer + dz) % layers
+
+            @pl.when(q + 4 * source < chunks)
+            def _():
+                far_copy(q, source, layer).wait_recv()
+                held_ref[at, :] += far_ref[source, q]
+
+    def finish(pair):
+        count = count_ref[0]
+        index = lax.broadcasted_iota(jnp.int32, table, 0)
+        lane_at = lax.broadcasted_iota(jnp.int32, table, 1)
+        imaginary = lane_at >= both_waves
+        order = pair * both_waves + jnp.where(imaginary, lane_at - both_waves, lane_at)
+        places = jnp.where(index < tiny, index, (index - tiny) * tiny)
+        places = jnp.where(index < first, places, (index - first) * BLOCK)
+        phases = (places * order).astype(F32)
+        size = count.astype(F32)
+        phases = phases - jnp.floor(phases / size) * size
+        angles = 2.0 * math.pi * phases / size
+        cosine, sine = jnp.cos(angles), jnp.sin(angles)
+        weights = jnp.where(order == 0, 1.0, 2.0) * jnp.where(2 * order < count, 1.0, 0.0)
+        coarse_c = jnp.where(imaginary, -sine, cosine) * weights
+        coarse_s = jnp.where(imaginary, cosine, sine) * weights
+        for b in range(middle):
+            turn_c, turn_s = cosine[tiny + b:tiny + b + 1], sine[tiny + b:tiny + b + 1]
+            fcos_ref[pl.ds(b * tiny, tiny), :] = cosine[:tiny] * turn_c - sine[:tiny] * turn_s
+            fsin_ref[pl.ds(b * tiny, tiny), :] = sine[:tiny] * turn_c + cosine[:tiny] * turn_s
+
+        collect(2 * pair, 0)
+        collect(2 * pair + 1, 1)
+        even = held_ref[pl.ds(0, both_waves, stride=2), :]
+        odd = held_ref[pl.ds(1, both_waves, stride=2), :]
+        half = columns // 2
+        basis = basis_ref[...]
+        top = jnp.concatenate((basis, basis), axis=1)
+        levels_both = jnp.concatenate((top, jnp.concatenate((basis, -basis), axis=1)), axis=0)
+        real = jnp.concatenate((even[:, :half], odd[:, :half]), axis=1)
+        imag = jnp.concatenate((even[:, half:], odd[:, half:]), axis=1)
+        high, low = split(dot3(jnp.concatenate((real, imag), axis=0), levels_both))
+        for b in range(points // BLOCK):
+            lookup = coarse_c[first + b:first + b + 1] * fcos_ref[...] - coarse_s[first + b:first + b + 1] * fsin_ref[...]
+            lookup_high, lookup_low = split(lookup)
+            temps = dot(jnp.concatenate((lookup_high, lookup_low), axis=0), high)
+            out_ref[pl.ds(b * BLOCK, BLOCK), :] += temps[:BLOCK] + temps[BLOCK:] + dot(lookup_high, low)
+
+    lag = min(5, chunks)
     ahead = 2
     for owner in range(ahead):
         receive(owner)
 
-    @pl.loop(0, chunks + 1)
+    @pl.loop(0, chunks + lag + 1)
     def _(t):
         @pl.when(t + ahead < chunks)
         def _():
@@ -259,37 +325,19 @@
         def _():
             compute(t)
 
-        @pl.when(t >= 1)
+        @pl.when(jnp.logical_and(t >= 1, t <= chunks))
         def _():
             merge_near(t - 1)
 
-        @pl.when(t >= lag)
+        @pl.when(jnp.logical_and(t >= lag, t < chunks + lag))
         def _():
             merge_side(t - lag)
 
-    @pl.loop(chunks + 1 - lag, chunks)
-    def _(q):
-        merge_side(q)
-
-    @pl.loop(0, chunks)
-    def _(q):
-        at = pl.ds(pl.multiple_of(q * part, part), part)
-
-        @pl.when(q + 4 * layer < chunks)
-        def _():
-            out_ref[at, :] = sums_ref[q, core, side, layer]
-
-        @pl.when(q + 4 * layer >= chunks)
-        def _():
-            out_ref[at, :] = jnp.zeros((part, columns), F32)
-
-        for dz in range(1, layers):
-            source = (layer + dz) % layers
-
-            @pl.when(q + 4 * source < chunks)
-            def _():
-                far_copy(q, source, layer).wait_recv()
-                out_ref[at, :] += far_ref[source, q]
+        late = t - lag - 2
+
+        @pl.when(jnp.logical_and(t >= lag + 2, late % 2 == 0))
+        def _():
+            finish(late // 2)
 
     for offset in others:
         target = other(offset)
@@ -318,7 +366,7 @@
                 far_copy(q, layer, (layer + dz) % layers).wait_send()
 
 
-def exchanged_sums(coefficients, legendre, n, draws):
+def exchanged_sums(coefficients, legendre, row_counts, basis, n, draws, points):
     waves, _, slots, columns = coefficients.shape
     own, _, every, rows = legendre.shape
     dense = jnp.transpose(coefficients, (0, 2, 1, 3)).reshape(waves * slots * 2, columns)
@@ -334,8 +382,13 @@
 
     return pl.pallas_call(
         body,
-        out_shape=jax.ShapeDtypeStruct((2 * waves, columns), F32),
-        in_specs=[pl.BlockSpec(memory_space=pl.ANY), pl.BlockSpec(memory_space=pltpu.VMEM)],
+        out_shape=jax.ShapeDtypeStruct((points, 2 * basis.shape[1]), F32),
+        in_specs=[
+            pl.BlockSpec(memory_space=pltpu.SMEM),
+            pl.BlockSpec(memory_space=pl.ANY),
+            pl.BlockSpec(memory_space=pltpu.VMEM),
+            pl.BlockSpec(memory_space=pltpu.VMEM),
+        ],
         out_specs=pl.BlockSpec(memory_space=pltpu.VMEM),
         scratch_shapes=[
             pltpu.VMEM(dense.shape, BF16),
@@ -346,6 +399,9 @@
             pltpu.VMEM((chunks, 2, layers, width, columns), F32),
             pltpu.VMEM((chunks, layers, width, columns), F32),
             pltpu.VMEM((layers, chunks, width, columns), F32),
+            pltpu.VMEM((2 * width, columns), F32),
+            pltpu.VMEM((BLOCK, 4 * own), F32),
+            pltpu.VMEM((BLOCK, 4 * own), F32),
             dma, dma((n,)), dma((n,)), dma((n,)),
             dma((chunks,)), dma((chunks,)),
             dma((chunks,)), dma((chunks,)),
@@ -355,53 +411,16 @@
             collective_id=0, has_side_effects=True, vmem_limit_bytes=58 * 1024 * 1024
         ),
         name="exchanged_sums",
-    )(dense, legs)
-
-
-def row_kernel(
-    count_ref, spectra_ref, basis_ref, absorb_ref, peak_ref, width_ref, out_ref,
-    fcos_ref, fsin_ref, ccos_ref, csin_ref, high_ref, low_ref, rhigh_ref, rlow_ref,
-):
+    )(row_counts, dense, legs, basis)
+
+
+def row_kernel(count_ref, temps_ref, absorb_ref, peak_ref, width_ref, out_ref, rhigh_ref, rlow_ref):
     step = pl.program_id(0)
-    waves = fcos_ref.shape[1]
     levels = absorb_ref.shape[1]
-    points = fcos_ref.shape[0]
-    tiny = 16
-    middle = points // tiny
+    points = temps_ref.shape[0]
 
     @pl.when(step == 0)
     def _():
-        count = count_ref[0].astype(F32)
-        table = (tiny + middle + ccos_ref.shape[0], waves)
-        index = lax.broadcasted_iota(jnp.int32, table, 0)
-        order = lax.broadcasted_iota(jnp.int32, table, 1)
-        places = jnp.where(index < tiny, index, (index - tiny) * tiny)
-        places = jnp.where(index < tiny + middle, places, (index - tiny - middle) * points)
-        phases = (places * order).astype(F32)
-        phases = phases - jnp.floor(phases / count) * count
-        angles = 2.0 * math.pi * phases / count
-        cosine, sine = jnp.cos(angles), jnp.sin(angles)
-        weights = jnp.where(order == 0, 1.0, 2.0) * jnp.where(2 * order < count_ref[0], 1.0, 0.0)
-        first = tiny + middle
-        ccos_ref[...] = (cosine * weights)[first:]
-        csin_ref[...] = (sine * weights)[first:]
-        for b in range(middle):
-            turn_c, turn_s = cosine[tiny + b:tiny + b + 1], sine[tiny + b:tiny + b + 1]
-            fcos_ref[pl.ds(b * tiny, tiny), :] = cosine[:tiny] * turn_c - sine[:tiny] * turn_s
-            fsin_ref[pl.ds(b * tiny, tiny), :] = sine[:tiny] * turn_c + cosine[:tiny] * turn_s
-
-        even = spectra_ref[pl.ds(0, waves, stride=2), :]
-        odd = spectra_ref[pl.ds(1, waves, stride=2), :]
-        half = even.shape[1] // 2
-        real = jnp.concatenate((even[:, :half], odd[:, :half]), axis=1)
-        imag = jnp.concatenate((even[:, half:], odd[:, half:]), axis=1)
-        basis = basis_ref[...]
-        top = jnp.concatenate((basis, basis), axis=1)
-        wide = jnp.concatenate((top, jnp.concatenate((basis, -basis), axis=1)), axis=0)
-        for index, piece in enumerate((real, imag)):
-            high, low = split(dot3(piece, wide))
-            high_ref[pl.ds(index * waves, waves), :] = high
-            low_ref[pl.ds(index * waves, waves), :] = low
         height = lax.broadcasted_iota(jnp.int32, rlow_ref.shape, 0)
         offsets = (height - peak_ref[...]).astype(F32) / width_ref[...]
         shape = jnp.exp(-offsets * offsets)
@@ -410,17 +429,7 @@
         rhigh_ref[pl.ds(levels, levels), :] = high
         rlow_ref[...] = low
 
-    base_c = ccos_ref[pl.ds(step, 1), :]
-    base_s = csin_ref[pl.ds(step, 1), :]
-    fine_c = fcos_ref[...]
-    fine_s = fsin_ref[...]
-    cosine = base_c * fine_c - base_s * fine_s
-    sine = -(base_s * fine_c + base_c * fine_s)
-    lookup_high, lookup_low = split(jnp.concatenate((cosine, sine), axis=1))
-    high = high_ref[...]
-    temps = dot(lookup_high, high) + dot(lookup_low, high) + dot(lookup_high, low_ref[...])
-    temps = jnp.concatenate((temps[:, :levels], temps[:, levels:]), axis=0)
-
+    temps = jnp.concatenate((temps_ref[:, :levels], temps_ref[:, levels:]), axis=0)
     source = jnp.exp(0.5 * temps)
     layers = absorb_ref[...] * source
     before = lax.broadcasted_iota(jnp.int32, (2 * levels, levels), 0) % levels
@@ -438,12 +447,9 @@
     out_ref[0, 1] = bright[points:]
 
 
-def synthesize_row(spectra, row_counts, basis, absorb, peak_level, width, points):
-    waves = spectra.shape[0] // 2
+def radiate_row(temps, row_counts, absorb, peak_level, width):
+    points = temps.shape[0]
     levels, channels = absorb.shape[0], width.shape[0]
-    columns = spectra.shape[1]
-    steps = points // FINE
-    coarse = -(-steps // 8) * 8
 
     def whole(*shape):
         return pl.BlockSpec(shape, lambda i, *_: (0,) * len(shape))
@@ -453,28 +459,35 @@
         out_shape=jax.ShapeDtypeStruct((1, 2, points, channels), F32),
         grid_spec=pltpu.PrefetchScalarGridSpec(
             num_scalar_prefetch=1,
-            grid=(steps,),
+            grid=(points // FINE,),
             in_specs=[
-                whole(2 * waves, columns),
-                whole(*basis.shape),
+                pl.BlockSpec((FINE, 2 * levels), lambda i, *_: (i, 0)),
                 whole(1, levels),
                 whole(1, channels),
                 whole(1, channels),
             ],
             out_specs=pl.BlockSpec((1, 2, FINE, channels), lambda i, *_: (0, 0, i, 0)),
             scratch_shapes=[
-                pltpu.VMEM((FINE, waves), F32),
-                pltpu.VMEM((FINE, waves), F32),
-                pltpu.VMEM((coarse, waves), F32),
-                pltpu.VMEM((coarse, waves), F32),
-                pltpu.VMEM((2 * waves, 2 * levels), BF16),
-                pltpu.VMEM((2 * waves, 2 * levels), BF16),
                 pltpu.VMEM((2 * levels, channels), BF16),
                 pltpu.VMEM((levels, channels), BF16),
             ],
         ),
         name="row_synthesis",
-    )(row_counts, spectra, basis, absorb[None, :], peak_level[None, :], width[None, :])
+    )(row_counts, temps, absorb[None, :], peak_level[None, :], width[None, :])
+
+
+def row_temperatures(spectra, row_count, basis, points):
+    waves = spectra.shape[0] // 2
+    orders = jnp.arange(waves, dtype=jnp.int32)
+    places = jnp.arange(points, dtype=jnp.int32)
+    phases = places[:, None] * orders[None, :] % row_count
+    angles = 2.0 * math.pi * phases.astype(F32) / row_count.astype(F32)
+    weights = jnp.where(orders == 0, 1.0, 2.0) * (2 * orders < row_count).astype(F32)
+    parts = spectra.reshape(waves, 2, 2, basis.shape[0])
+    fields = jnp.einsum("km,mpc->pkc", weights * jnp.cos(angles), parts[:, :, 0], precision=PRECISE)
+    fields = fields - jnp.einsum("km,mpc->pkc", weights * jnp.sin(angles), parts[:, :, 1], precision=PRECISE)
+    fields = jnp.einsum("pkc,cl->pkl", fields, basis, precision=PRECISE)
+    return jnp.concatenate((fields[0] + fields[1], fields[0] - fields[1]), axis=1)
 
 
 def moved_coefficients(coefficients, legendre):
@@ -495,10 +508,10 @@
     fits = n == rows and n % 8 == 0 and 128 % n == 0 and every == n * slots and columns == 128
     fits = fits and (128 // n) % 8 == 0 and own % (128 // n) == 0 and slots % 4 == 0
     if fits and (slots * 128 // n) % 16 == 0 and 2 * waves >= 2 * slots * n:
-        spectra = exchanged_sums(coefficients, legendre, n, draws)
+        temps = exchanged_sums(coefficients, legendre, row_counts, basis, n, draws, NLON)
     else:
-        spectra = moved_coefficients(coefficients, legendre)
-    return synthesize_row(spectra, row_counts, basis, absorb, peak_level, width, NLON)
+        temps = row_temperatures(moved_coefficients(coefficients, legendre), row_counts[0], basis, NLON)
+    return radiate_row(temps, row_counts, absorb, peak_level, width)
 
 
 def solution(mesh):

time: 99.4 us -> 99.3 us (level)
  the two profiles are of different devices: /device:TPU:0 before, /device:TPU:26 now
where the time goes in v4:
time: 99.3 us; the launch traced here: 99 us
  Pallas kernels  98.4 us (99%)
    pallas_call x1, Pallas kernels, exchanged_sums(): pl.pallas_call(body, out_shape=jax.ShapeDtypeStruct((points, 2 * basis.sh...  91.8 us
    pallas_call x1, Pallas kernels, radiate_row(): pl.pallas_call(row_kernel, out_shape=jax.ShapeDtypeStruct((1, 2, points,...  6.54 us

profile of v4, /device:TPU:26, one launch (start us, length us, event | category | flops | bytes accessed | tf_op | source)
XLA Modules:
  0.0 99.0 jit_solution(7874050186124233168)
XLA Ops:
  0.7 91.8 %exchanged_sums.1.temps_ref = f32[1280,256]{1,0:T(8,128)} custom-call(s32[1]{0:T(128)S(6)} %copy.8.refs_0_.count_ref, bf16[25600,128]{1,0:T(8,128)(2,1)} %bitcast.9, f32[1280,320]{1,0:T(8,128)} %bitcast.10, f32[64,128]{1,0:T(8,128)} %refs_3_.1), custom_call_target="tpu_custom_call" | custom-call | tf_op jit(solution)/shard_map/exchanged_sums/pallas_call | solution.py:383
  92.5 6.5 %row_synthesis.1 = f32[1,2,1280,512]{3,2,1,0:T(8,128)} custom-call(s32[1]{0:T(128)S(6)} %copy.8.refs_0_.count_ref, f32[1280,256]{1,0:T(8,128)} %exchanged_sums.1.temps_ref, f32[1,128]{1,0:T(1,128)} %bitcast.13, s32[1,512]{1,0:T(1,128)} %bitcast.11, f32[1,512]{1,0:T(1,128)} %bitcast.12), custom_call_target="tpu_custom_call" | custom-call | tf_op jit(solution)/shard_map/row_synthesis/pallas_call | solution.py:457

commit v5 on v3

--- a/solution.py
+++ b/solution.py
@@ -9,7 +9,7 @@
 from jax.sharding import PartitionSpec as P
 
 NLON = 1280
-FINE = 128
+FINE = 256
 
 PRECISE = lax.Precision.HIGHEST
 F32 = jnp.float32
@@ -244,7 +244,7 @@
             for dz in range(1, layers):
                 far_copy(q, layer, (layer + dz) % layers).start()
 
-    lag = min(7, chunks)
+    lag = min(5, chunks)
     ahead = 2
     for owner in range(ahead):
         receive(owner)
@@ -417,8 +417,8 @@
     cosine = base_c * fine_c - base_s * fine_s
     sine = -(base_s * fine_c + base_c * fine_s)
     lookup_high, lookup_low = split(jnp.concatenate((cosine, sine), axis=1))
-    high = high_ref[...]
-    temps = dot(lookup_high, high) + dot(lookup_low, high) + dot(lookup_high, low_ref[...])
+    temps = dot(jnp.concatenate((lookup_high, lookup_low), axis=0), high_ref[...])
+    temps = temps[:points] + temps[points:] + dot(lookup_high, low_ref[...])
     temps = jnp.concatenate((temps[:, :levels], temps[:, levels:]), axis=0)
 
     source = jnp.exp(0.5 * temps)

time: 99.4 us -> 96.6 us (0.972)
  Pallas kernels: 97.7 us -> 95.8 us
    pallas_call x1, Pallas kernels: 14.4 us -> 12.5 us  [synthesize_row(): pl.pallas_call(row_kernel, out_shape=jax.ShapeDtypeStruct((1, 2, points,...]
where the time goes in v5:
time: 96.6 us; the launch traced here: 96.5 us
  Pallas kernels  95.8 us (99%)
    pallas_call x1, Pallas kernels, exchanged_sums(): pl.pallas_call(body, out_shape=jax.ShapeDtypeStruct((2 * waves, columns),...  83.3 us
    pallas_call x1, Pallas kernels, synthesize_row(): pl.pallas_call(row_kernel, out_shape=jax.ShapeDtypeStruct((1, 2, points,...  12.5 us

profile of v5, /device:TPU:0, one launch (start us, length us, event | category | flops | bytes accessed | tf_op | source)
XLA Modules:
  0.0 96.5 jit_solution(9779804255894694126)
XLA Ops:
  0.7 83.3 %exchanged_sums.1.spectra_ref = f32[1280,128]{1,0:T(8,128)} custom-call(bf16[25600,128]{1,0:T(8,128)(2,1)} %bitcast.9, f32[1280,320]{1,0:T(8,128)} %bitcast.10), custom_call_target="tpu_custom_call" | custom-call | tf_op jit(solution)/shard_map/exchanged_sums/pallas_call | solution.py:335
  83.9 12.5 %row_synthesis.1 = f32[1,2,1280,512]{3,2,1,0:T(8,128)} custom-call(s32[1]{0:T(128)S(6)} %copy.8.count_ref, f32[1280,128]{1,0:T(8,128)} %exchanged_sums.1.spectra_ref, f32[64,128]{1,0:T(8,128)} %basis_ref.1, f32[1,128]{1,0:T(1,128)} %bitcast.13, s32[1,512]{1,0:T(1,128)} %bitcast.11, f32[1,512]{1,0:T(1,128)} %bitcast.12), custom_call_target="tpu_custom_call" | custom-call | tf_op jit(solution)/shard_map/row_synthesis/pallas_call | solution.py:451
